TPU v7x, 512 devices: a whole 4x8x8 slice. The times are simulated.
512 devices in a mesh: dp: 16 (over y, core), seq: 32 (over x, z).
Axes of the slice: x: 4, y: 8, z: 8, core: 2. Of those that a mesh axis runs over, the one named last changes fastest.
Arguments:
- queries: bfloat16 [16, 4096, 2048], P('dp', 'seq'), may hold values from -40 to 40, as said below
- keys: bfloat16 [16, 4096, 2048], P('dp', 'seq'), may hold values from -40 to 40, as said below
- values: bfloat16 [16, 4096, 2048], P('dp', 'seq'), may hold values from -40 to 40, as said below
- gain: float32 [2048], replicated, may hold values from 0.1 to 1.9
- cotangent: bfloat16 [16, 4096, 2048], P('dp', 'seq'), may hold values from -240 to 240, as said below
Outputs:
- output: bfloat16 [16, 4096, 2048], P('dp', 'seq')
- grad_query: bfloat16 [16, 4096, 2048], P('dp', 'seq')
- grad_key: bfloat16 [16, 4096, 2048], P('dp', 'seq')
- grad_value: bfloat16 [16, 4096, 2048], P('dp', 'seq')
- gain_grad: float32 [2048], replicated
Inputs may be any that keep to these rules, and one draw needn't show every extreme that they name: queries: independent entries with row and feature scales. keys: independent entries with row and feature scales. values: independent entries with row and feature scales. cotangent: independent entries with row and feature scales.
All inputs are finite; a program needn't handle non-finite values.
Results may differ from a plain program's by a relative error of at most 0.0058.
Values may be sent and summed in bfloat16 or wider, within the bound.
A program may use at most 64 MiB of HBM per device.

v0:
```python
import jax
import jax.numpy as jnp
from jax import lax
from jax.sharding import PartitionSpec as P

HEADS = 16


EPSILON = 1e-06


def prefix_swapped(state_block, reverse_order):
    device_count = lax.axis_size("seq")
    flat_state = state_block.reshape(1, -1)
    columns = lax.all_to_all(flat_state, "seq", split_axis=1, concat_axis=0, tiled=True)
    device_rank = jnp.arange(device_count)
    if reverse_order:
        triangle = device_rank[None, :] > device_rank[:, None]
    else:
        triangle = device_rank[None, :] < device_rank[:, None]
    summed = jnp.dot(triangle.astype(jnp.float32), columns, precision=lax.Precision.HIGHEST)
    summed_half = summed.astype(jnp.bfloat16)
    returned = lax.all_to_all(summed_half, "seq", split_axis=0, concat_axis=1, tiled=True)
    return returned.reshape(state_block.shape)


def per_device(queries, keys, values, gain, cotangent):
    row_count = queries.shape[1]
    feature_count = queries.shape[2]
    head_size = feature_count // HEADS
    scaling = head_size ** (-0.5)
    query_rows = queries[0].reshape(row_count, HEADS, head_size)
    key_rows = keys[0].reshape(row_count, HEADS, head_size)
    value_rows = values[0].reshape(row_count, HEADS, head_size)
    kv_local = jnp.einsum("thd,the->hde", key_rows, value_rows, preferred_element_type=jnp.float32)
    prefix_half = prefix_swapped(kv_local, False)
    position = jnp.arange(row_count)
    causal_mask = (position[:, None] >= position[None, :]).astype(jnp.float32)
    scores = (
        jnp.einsum("thd,uhd->htu", query_rows, key_rows, preferred_element_type=jnp.float32)
        * scaling
        * causal_mask
    ).astype(jnp.bfloat16)
    attended = jnp.einsum("htu,uhe->the", scores, value_rows, preferred_element_type=jnp.float32)
    attended = attended + scaling * jnp.einsum(
        "thd,hde->the", query_rows, prefix_half, preferred_element_type=jnp.float32
    )
    attended = attended.reshape(row_count, feature_count)
    root_mean = jnp.sqrt(jnp.mean(attended * attended, axis=-1, keepdims=True) + EPSILON)
    normalized = attended / root_mean
    output = (gain * normalized).astype(jnp.bfloat16)[None]
    upstream = cotangent[0].astype(jnp.float32)
    partial_gain = jnp.sum(upstream * normalized, axis=0)
    total_gain = lax.psum(partial_gain, ("dp", "seq"))
    gain_grad = total_gain / lax.axis_size("dp")
    scaled = upstream * gain
    inner_mean = jnp.mean(scaled * normalized, axis=-1, keepdims=True)
    grad_attn = (
        ((scaled - normalized * inner_mean) / root_mean)
        .astype(jnp.bfloat16)
        .reshape(row_count, HEADS, head_size)
    )
    local_grads = scaling * jnp.einsum(
        "thd,the->hde", query_rows, grad_attn, preferred_element_type=jnp.float32
    )
    suffix_half = prefix_swapped(local_grads, True)
    grad_scores = (
        jnp.einsum("the,uhe->htu", grad_attn, value_rows, preferred_element_type=jnp.float32)
        * causal_mask
    ).astype(jnp.bfloat16)
    grad_query = scaling * (
        jnp.einsum("htu,uhd->thd", grad_scores, key_rows, preferred_element_type=jnp.float32)
        + jnp.einsum("the,hde->thd", grad_attn, prefix_half, preferred_element_type=jnp.float32)
    )
    grad_key = scaling * jnp.einsum(
        "htu,thd->uhd", grad_scores, query_rows, preferred_element_type=jnp.float32
    ) + jnp.einsum("uhe,hde->uhd", value_rows, suffix_half, preferred_element_type=jnp.float32)
    grad_value = jnp.einsum(
        "htu,the->uhe", scores, grad_attn, preferred_element_type=jnp.float32
    ) + jnp.einsum("uhd,hde->uhe", key_rows, suffix_half, preferred_element_type=jnp.float32)
    out_shape = (1, row_count, feature_count)
    return (
        output,
        grad_query.reshape(out_shape).astype(jnp.bfloat16),
        grad_key.reshape(out_shape).astype(jnp.bfloat16),
        grad_value.reshape(out_shape).astype(jnp.bfloat16),
        gain_grad,
    )


def solution(mesh):
    return jax.shard_map(
        per_device,
        mesh=mesh,
        in_specs=(
            P("dp", "seq", None),
            P("dp", "seq", None),
            P("dp", "seq", None),
            P(),
            P("dp", "seq", None),
        ),
        out_specs=(
            P("dp", "seq", None),
            P("dp", "seq", None),
            P("dp", "seq", None),
            P("dp", "seq", None),
            P(),
        ),
        check_vma=False,
    )
```

profile of v0, /device:TPU:1, one launch (start us, length us, event | category | flops | bytes accessed | tf_op | source)
XLA Modules:
  0.0 252.3 jit_solution(6267400844076144092)
XLA Ops:
  0.6 1.1 copy.128
  1.8 0.0 copy-start.13
  1.8 0.5 copy.92
  2.3 0.0 copy-start.3
  2.3 0.6 copy-done.13
  2.8 0.1 copy.129
  2.9 0.1 copy-done.3
  3.1 0.3 fusion.26
  3.4 38.4 %all_to_all.58 = f32[1,32,8192]{2,0,1:T(1,128)S(1)} all-to-all(f32[1,32,8192]{2,0,1:T(1,128)S(1)} %bitcast.94), channel_id=1, replica_groups=mesh['dp'=16,'seq'=32] {'seq'}, dimensions={1} | all-to-all | bytes 2097152 | tf_op jit(solution)/shard_map/all_to_all | solution.py:15
  41.7 1.3 fusion
  43.0 0.5 broadcast.107
  43.5 1.0 reduce.3
  44.6 1.2 reshape.208
  45.7 8.5 %all-to-all-start.1 = ((bf16[32,2,4096]{2,1,0:T(2,128)(2,1)}), bf16[32,2,4096]{2,1,0:T(2,128)(2,1)S(1)}, u32[]{:S(2)}, u32[]{:S(2)}) async-start(bf16[32,2,4096]{2,1,0:T(2,128)(2,1)} %reshape.208), calls=%async_computation.1 | async-start | bytes 1048576 | tf_op jit(solution)/shard_map/all_to_all | solution.py:23
  54.2 0.0 copy-start.9
  54.2 0.1 copy.127
  54.3 0.9 copy-done.9
  55.3 1.2 copy.99
  56.5 0.5 fusion.10
  57.0 1.5 convolution_bitcast_fusion.3
  58.5 9.7 %all-to-all-done.1 = bf16[32,2,4096]{2,1,0:T(2,128)(2,1)S(1)} async-done(((bf16[32,2,4096]{2,1,0:T(2,128)(2,1)}), bf16[32,2,4096]{2,1,0:T(2,128)(2,1)S(1)}, u32[]{:S(2)}, u32[]{:S(2)}) %all-to-all-start.1) | async-done | bytes 524320 | tf_op jit(solution)/shard_map/all_to_all | solution.py:23
  68.2 0.5 reshape.209
  68.7 4.0 %reduce.1 = bf16[32,8192]{1,0:T(8,128)(2,1)} reduce(bf16[32,1,8192]{2,1,0:T(2,128)(2,1)S(1)} %reshape.209, bf16[]{:T(256)} %constant.19), dimensions={1}, to_apply=%all_to_all.48.reduce_sub_computation | reduce | bytes 1048578 | tf_op jit(solution)/shard_map/all_to_all | solution.py:23
  72.7 1.3 reshape.200
  74.0 0.0 copy-start
  74.0 1.9 multiply_reduce_fusion
  75.9 0.0 copy-start.10
  75.9 0.0 copy-start.15
  75.9 1.4 copy.100
  77.3 1.7 fusion.20
  79.0 0.3 divide_convert_fusion
  79.4 1.3 fusion.3
  80.7 2.5 %copy.108 = f32[16,128,128]{2,1,0:T(8,128)} copy(f32[16,128,128]{1,2,0:T(8,128)} %fusion.3) | data formatting | bytes 2097152 | tf_op jit(solution)/shard_map/mul | solution.py:63
  83.2 8.1 %all-to-all-start.2 = ((f32[1,32,8192]{2,0,1:T(1,128)}), f32[1,32,8192]{2,0,1:T(1,128)}, u32[]{:S(2)}, u32[]{:S(2)}) async-start(f32[1,32,8192]{2,0,1:T(1,128)} %bitcast.93), calls=%async_computation.2 | async-start | bytes 2097152 | tf_op jit(solution)/shard_map/all_to_all | solution.py:15
  91.3 0.0 copy-start.4
  91.3 0.5 fusion.11
  91.9 0.5 copy-done.4
  92.4 0.5 convolution_bitcast_fusion.2
  92.9 0.3 copy-done.2
  93.2 0.4 copy-done.1
  93.6 1.1 fusion.9
  94.7 21.5 %all-to-all-done.2 = f32[1,32,8192]{2,0,1:T(1,128)} async-done(((f32[1,32,8192]{2,0,1:T(1,128)}), f32[1,32,8192]{2,0,1:T(1,128)}, u32[]{:S(2)}, u32[]{:S(2)}) %all-to-all-start.2) | async-done | bytes 1048608 | tf_op jit(solution)/shard_map/all_to_all | solution.py:15
  116.2 3.2 %fusion.1 = bf16[32,1,8192]{2,0,1:T(8,128)(2,1)} fusion(f32[1,32,8192]{2,0,1:T(1,128)} %all-to-all-done.2), kind=kOutput, calls=%fused_computation.3 | convolution fusion | flops 100926464 | bytes 1572864 | tf_op jit(solution)/shard_map/dot_general | solution.py:21
  119.4 2.7 %reduce.4 = bf16[32,8192]{1,0:T(8,128)(2,1)} reduce(bf16[32,1,8192]{2,0,1:T(8,128)(2,1)} %fusion.1, bf16[]{:T(256)} %broadcast.107), dimensions={1}, to_apply=%copy.110.reduce_sub_computation | reduce | bytes 1048578 | tf_op jit(solution)/shard_map/all_to_all | solution.py:23
  122.1 2.2 reshape.210
  124.3 8.3 %all-to-all-start.3 = ((bf16[32,2,4096]{2,1,0:T(2,128)(2,1)}), bf16[32,2,4096]{2,1,0:T(2,128)(2,1)}, u32[]{:S(2)}, u32[]{:S(2)}) async-start(bf16[32,2,4096]{2,1,0:T(2,128)(2,1)} %reshape.210), calls=%async_computation.3 | async-start | bytes 1048576 | tf_op jit(solution)/shard_map/all_to_all | solution.py:23
  132.6 2.4 fusion.4
  135.0 1.4 copy.98
  136.3 1.0 copy.116
  137.4 99.2 %psum.7 = f32[2048]{0:T(1024)S(1)} all-reduce(f32[2048]{0:T(1024)S(1)} %get-tuple-element.25), channel_id=1, replica_groups=mesh['dp'=16,'seq'=32] {'dp','seq'}, use_global_device_ids=true, to_apply=%region_3.0 | all-reduce | flops 2048 | bytes 16384 | tf_op jit(solution)/shard_map/psum | solution.py:54
  236.5 0.6 broadcast_multiply_fusion
  237.2 0.3 fusion.34
  237.4 0.9 copy-done.7
  238.4 1.0 multiply_convert_fusion
  239.4 0.0 all-to-all-done.3
  239.4 3.6 %reshape.211 = bf16[32,1,8192]{2,1,0:T(2,128)(2,1)S(1)} reshape(bf16[32,2,4096]{2,1,0:T(2,128)(2,1)} %all-to-all-done.3) | data formatting | bytes 1048576
  243.0 4.0 %reduce.2 = bf16[32,8192]{1,0:T(8,128)(2,1)} reduce(bf16[32,1,8192]{2,1,0:T(2,128)(2,1)S(1)} %reshape.211, bf16[]{:T(256)} %constant.19), dimensions={1}, to_apply=%all_to_all.53.reduce_sub_computation | reduce | bytes 1048578 | tf_op jit(solution)/shard_map/all_to_all | solution.py:23
  246.9 1.3 reshape.203
  248.2 0.5 fusion.13
  248.8 0.7 copy-done.6
  249.5 0.5 fusion.12
  249.9 0.3 copy.113
  250.2 1.0 copy.117
  251.2 1.0 copy.118
  (21 shorter events, 0.1 us)
Async XLA Ops:
  1.8 1.0 copy-start.13
  2.3 0.8 copy-start.3
  45.7 8.5 %copy-start.14 = (bf16[1,128,2048]{2,1,0:T(8,128)(2,1)S(1)}, bf16[1,128,2048]{2,1,0:T(8,128)(2,1)}, u32[]{:S(2)}) copy-start(bf16[1,128,2048]{2,1,0:T(8,128)(2,1)} %param.5) | copy-start | bytes 1572868
  45.7 22.5 %all-to-all-start.1 = ((bf16[32,2,4096]{2,1,0:T(2,128)(2,1)}), bf16[32,2,4096]{2,1,0:T(2,128)(2,1)S(1)}, u32[]{:S(2)}, u32[]{:S(2)}) async-start(bf16[32,2,4096]{2,1,0:T(2,128)(2,1)} %reshape.208), calls=%async_computation.1 | async-start | bytes 1048576 | tf_op jit(solution)/shard_map/all_to_all | solution.py:23
  54.2 1.0 copy-start.9
  57.0 1.6 copy-start.11
  74.0 1.9 copy-start
  75.9 1.4 copy-start.10
  75.9 1.4 copy-start.15
  77.3 1.7 copy-start.5
  83.2 32.9 %all-to-all-start.2 = ((f32[1,32,8192]{2,0,1:T(1,128)}), f32[1,32,8192]{2,0,1:T(1,128)}, u32[]{:S(2)}, u32[]{:S(2)}) async-start(f32[1,32,8192]{2,0,1:T(1,128)} %bitcast.93), calls=%async_computation.2 | async-start | bytes 2097152 | tf_op jit(solution)/shard_map/all_to_all | solution.py:15
  91.3 1.0 copy-start.4
  92.4 0.8 copy-start.2
  92.4 1.2 copy-start.1
  124.3 115.0 %all-to-all-start.3 = ((bf16[32,2,4096]{2,1,0:T(2,128)(2,1)}), bf16[32,2,4096]{2,1,0:T(2,128)(2,1)}, u32[]{:S(2)}, u32[]{:S(2)}) async-start(bf16[32,2,4096]{2,1,0:T(2,128)(2,1)} %reshape.210), calls=%async_computation.3 | async-start | bytes 1048576 | tf_op jit(solution)/shard_map/all_to_all | solution.py:23
  135.0 1.4 copy-start.8
  136.3 100.8 %copy-start.12 = (bf16[16,128,128]{2,1,0:T(8,128)(2,1)S(1)}, bf16[16,128,128]{2,1,0:T(8,128)(2,1)}, u32[]{:S(2)}) copy-start(bf16[16,128,128]{2,1,0:T(8,128)(2,1)} %copy-done.11) | copy-start | bytes 1572868
  237.2 1.2 copy-start.7
  248.2 1.2 copy-start.6
where the time goes:
time: 254 us; the launch traced here: 252 us
  blocking collectives  138 us (54%)
  waiting for transfers between devices  31.1 us (12%)
  local copies, waits for them, and re-layouts  26.8 us (11%)
  starting transfers between devices  24.8 us (10%)
  matrix products  15.8 us (6%)
  other arithmetic  15.3 us (6%)
    psum x1, blocking collectives, per_device(): total_gain = lax.psum(partial_gain, ('dp', 'seq'))  99.2 us
    all_to_all x1, blocking collectives, prefix_swapped(): lax.all_to_all(flat_state, 'seq', split_axis=1, concat_axis=0, tiled=True)  38.4 us
    all_to_all x1, waiting for transfers between devices, prefix_swapped(): lax.all_to_all(flat_state, 'seq', split_axis=1, concat_axis=0, tiled=True)  21.5 us
    all_to_all x2, starting transfers between devices, prefix_swapped(): lax.all_to_all(summed_half, 'seq', split_axis=0, concat_axis=1, tiled=True)  16.7 us
    unnamed x42, local copies, waits for them, and re-layouts  16.5 us
    all_to_all x4, other arithmetic, prefix_swapped(): lax.all_to_all(summed_half, 'seq', split_axis=0, concat_axis=1, tiled=True)  11.6 us
    all_to_all x2, waiting for transfers between devices, prefix_swapped(): lax.all_to_all(summed_half, 'seq', split_axis=0, concat_axis=1, tiled=True)  9.67 us
    all_to_all x1, starting transfers between devices, prefix_swapped(): lax.all_to_all(flat_state, 'seq', split_axis=1, concat_axis=0, tiled=True)  8.06 us
  transfers between devices with their start and end apart: 3, of which 2 were waited for; matrix products, arithmetic and copies ran while one was open for 5% of the time, Pallas kernels for 0%

commit v1 on v0

v1 whole, which is shorter than its diff:
```python
import functools

import jax
import jax.numpy as jnp
from jax import lax
from jax.experimental import pallas as pl
from jax.experimental.pallas import tpu as pltpu
from jax.sharding import PartitionSpec as P

HEADS = 16
HEAD = 128
EPSILON = 1e-06
RING = 8
UNROLL = 4
MESH = pl.DeviceIdType.MESH
F32 = jnp.float32
BF16 = jnp.bfloat16


def dot(a, b, ca, cb):
    return lax.dot_general(a, b, (((ca,), (cb,)), ((), ())), preferred_element_type=F32)


def heads_loop(body):
    @pl.loop(0, HEADS // UNROLL)
    def _(step):
        for inner in range(UNROLL):
            body(step * UNROLL + inner)


def kernel(
    n_seq,
    n_dp,
    q_hbm,
    k_hbm,
    v_hbm,
    gain_hbm,
    cot_hbm,
    out_hbm,
    gq_hbm,
    gk_hbm,
    gv_hbm,
    gg_hbm,
    q_ref,
    k_ref,
    v_ref,
    cot_ref,
    gain_ref,
    att_ref,
    score_ref,
    ga_ref,
    gk_part,
    gv_part,
    out_ref,
    gq_ref,
    gk_ref,
    gv_ref,
    send_a,
    recv_a,
    send_b,
    recv_b,
    send_c,
    recv_c,
    send_d,
    recv_d,
    gain_part,
    gain_r1,
    gain_s2,
    gain_r2,
    gain_r3,
    gain_out,
    load_sem,
    store_sem,
    send_sem,
    recv_sem,
    gain_send_sem,
    gain_recv_sem,
    own_sem,
):
    seq = lax.axis_index("seq")
    dp = lax.axis_index("dp")
    rows = HEADS * HEAD // n_seq
    tokens = q_ref.shape[0]
    features = HEADS * HEAD
    scaling = HEAD ** (-0.5)
    n_x = n_seq // RING
    grows = HEADS // n_dp

    def slot(p):
        return pl.ds(pl.multiple_of(p * rows, rows), rows)

    def cols(h):
        return pl.ds(pl.multiple_of(h * HEAD, HEAD), HEAD)

    loads = [
        pltpu.make_async_copy(k_hbm.at[0], k_ref, load_sem.at[0]),
        pltpu.make_async_copy(v_hbm.at[0], v_ref, load_sem.at[1]),
        pltpu.make_async_copy(q_hbm.at[0], q_ref, load_sem.at[2]),
        pltpu.make_async_copy(cot_hbm.at[0], cot_ref, load_sem.at[3]),
        pltpu.make_async_copy(gain_hbm, gain_ref, load_sem.at[4]),
    ]
    for load in loads:
        load.start()

    barrier = pltpu.get_barrier_semaphore()

    @pl.loop(1, n_seq)
    def _(k):
        peer = lax.rem(seq + k, n_seq)
        pl.semaphore_signal(barrier, inc=1, device_id={"seq": peer}, device_id_type=MESH)

    @pl.loop(1, n_dp)
    def _(k):
        peer = lax.rem(dp + k, n_dp)
        pl.semaphore_signal(barrier, inc=1, device_id={"dp": peer}, device_id_type=MESH)

    def peer_at(k):
        j = k // n_x
        half = (j + 1) // 2
        offset = jnp.where(lax.rem(j, 2) == 0, RING // 2 + half, RING // 2 - half)
        step = lax.rem(lax.rem(k, n_x) + 1, n_x)
        z = lax.rem(lax.rem(seq, RING) + offset, RING)
        x = lax.rem(seq // RING + step, n_x)
        return x * RING + z

    def exchange(src, dst, index):
        @pl.loop(0, n_seq - 1)
        def _(k):
            peer = peer_at(k)
            pltpu.make_async_remote_copy(
                src_ref=src.at[slot(peer)],
                dst_ref=dst.at[slot(seq)],
                send_sem=send_sem.at[index],
                recv_sem=recv_sem.at[index],
                device_id={"seq": peer},
                device_id_type=MESH,
            ).start()

        own = pltpu.make_async_copy(src.at[slot(seq)], dst.at[slot(seq)], own_sem.at[index])
        own.start()
        return own

    def descriptor(src, dst, index):
        part = pl.ds(0, (n_seq - 1) * rows)
        return pltpu.make_async_remote_copy(
            src_ref=src.at[part],
            dst_ref=dst.at[part],
            send_sem=send_sem.at[index],
            recv_sem=recv_sem.at[index],
            device_id={"seq": lax.rem(seq + 1, n_seq)},
            device_id_type=MESH,
        )

    position_t = lax.broadcasted_iota(jnp.int32, (tokens, tokens), 0)
    position_u = lax.broadcasted_iota(jnp.int32, (tokens, tokens), 1)
    causal = position_t >= position_u

    loads[0].wait()
    loads[1].wait()

    def state_of(h):
        c = cols(h)
        send_a[c, :] = dot(k_ref[:, c], v_ref[:, c], 0, 0).astype(BF16)

    heads_loop(state_of)
    pl.semaphore_wait(barrier, n_seq - 1 + n_dp - 1)
    own_a = exchange(send_a, recv_a, 0)

    loads[2].wait()
    loads[3].wait()
    loads[4].wait()

    def local_of(h):
        c = cols(h)
        raw = dot(q_ref[:, c], k_ref[:, c], 1, 1)
        score = jnp.where(causal, raw * scaling, 0.0).astype(BF16)
        score_ref[c, :] = score
        att_ref[:, c] = dot(score, v_ref[:, c], 1, 0)

    heads_loop(local_of)

    def scan(src, dst, reverse):
        def step(i, total):
            b = n_seq - 1 - i if reverse else i
            dst[slot(b), :] = total.astype(BF16)
            return total + src[slot(b), :].astype(F32)

        lax.fori_loop(0, n_seq, step, jnp.zeros((rows, HEAD), F32))

    own_a.wait()
    descriptor(send_a, recv_a, 0).wait_recv()
    scan(recv_a, send_b, False)
    own_b = exchange(send_b, recv_b, 1)
    own_b.wait()
    descriptor(send_b, recv_b, 1).wait_recv()

    def attend(step, carry):
        squares, inner = carry
        for k in range(UNROLL):
            h = step * UNROLL + k
            c = cols(h)
            att = att_ref[:, c] + scaling * dot(q_ref[:, c], recv_b[c, :], 1, 0)
            att_ref[:, c] = att
            squares = squares + att * att
            inner = inner + att * (cot_ref[:, c].astype(F32) * gain_ref[pl.ds(h, 1), :])
        return squares, inner

    zero = jnp.zeros((tokens, HEAD), F32)
    squares, inner = lax.fori_loop(0, HEADS // UNROLL, attend, (zero, zero))
    root = jnp.sqrt(jnp.sum(squares, axis=1, keepdims=True) / features + EPSILON)
    inverse = 1.0 / root
    mean = jnp.sum(inner, axis=1, keepdims=True) * inverse / features

    def normalize(h):
        c = cols(h)
        weight = gain_ref[pl.ds(h, 1), :]
        upstream = cot_ref[:, c].astype(F32)
        normalized = att_ref[:, c] * inverse
        out_ref[:, c] = (weight * normalized).astype(BF16)
        gain_part[h] = jnp.sum(upstream * normalized, axis=0, keepdims=True)
        grad = ((upstream * weight - normalized * mean) * inverse).astype(BF16)
        ga_ref[:, c] = grad
        send_c[c, :] = (scaling * dot(q_ref[:, c], grad, 0, 0)).astype(BF16)

    heads_loop(normalize)
    own_c = exchange(send_c, recv_c, 2)

    def gain_copy(src, dst, index, axis, peer):
        return pltpu.make_async_remote_copy(
            src_ref=src,
            dst_ref=dst,
            send_sem=gain_send_sem.at[index],
            recv_sem=gain_recv_sem.at[index],
            device_id={axis: peer},
            device_id_type=MESH,
        )

    def part(j):
        return pl.ds(j * grows, grows)

    @pl.loop(1, n_dp)
    def _(k):
        peer = lax.rem(dp + k, n_dp)
        gain_copy(gain_part.at[part(peer)], gain_r1.at[part(dp)], 0, "dp", peer).start()

    store_out = pltpu.make_async_copy(out_ref, out_hbm.at[0], store_sem.at[0])
    store_out.start()

    def grads(h):
        c = cols(h)
        grad = ga_ref[:, c]
        gs = jnp.where(causal, dot(grad, v_ref[:, c], 1, 1), 0.0).astype(BF16)
        query = dot(gs, k_ref[:, c], 1, 0) + dot(grad, recv_b[c, :], 1, 1)
        gq_ref[:, c] = (scaling * query).astype(BF16)
        gk_part[:, c] = scaling * dot(gs, q_ref[:, c], 0, 0)
        gv_part[:, c] = dot(score_ref[c, :], grad, 0, 0)

    heads_loop(grads)
    store_gq = pltpu.make_async_copy(gq_ref, gq_hbm.at[0], store_sem.at[1])
    store_gq.start()

    gain_r1[part(dp)] = gain_part[part(dp)]
    others = pl.ds(0, (n_dp - 1) * grows)
    first = gain_copy(gain_part.at[others], gain_r1.at[others], 0, "dp", lax.rem(dp + 1, n_dp))
    first.wait_recv()
    summed = jnp.zeros((grows, 1, HEAD), F32)
    for j in range(n_dp):
        summed = summed + gain_r1[pl.ds(j * grows, grows)]
    gain_s2[...] = summed

    @pl.loop(0, n_seq - 1)
    def _(k):
        peer = peer_at(k)
        gain_copy(gain_s2, gain_r2.at[pl.ds(seq * grows, grows)], 1, "seq", peer).start()

    own_c.wait()
    descriptor(send_c, recv_c, 2).wait_recv()
    scan(recv_c, send_d, True)
    own_d = exchange(send_d, recv_d, 3)

    gain_r2[pl.ds(seq * grows, grows)] = summed
    some = pl.ds(0, (n_seq - 1) * grows)
    second = gain_copy(gain_r2.at[some], gain_r2.at[some], 1, "seq", lax.rem(seq + 1, n_seq))
    second.wait_recv()

    def add(j, total):
        return total + gain_r2[pl.ds(j * grows, grows)]

    total = lax.fori_loop(0, n_seq, add, jnp.zeros((grows, 1, HEAD), F32)) / n_dp
    gain_r3[part(dp)] = total

    @pl.loop(1, n_dp)
    def _(k):
        peer = lax.rem(dp + k, n_dp)
        gain_copy(gain_r3.at[part(dp)], gain_r3.at[part(dp)], 2, "dp", peer).start()

    own_d.wait()
    descriptor(send_d, recv_d, 3).wait_recv()

    def finish(h):
        c = cols(h)
        suffix = recv_d[c, :]
        gk_ref[:, c] = (gk_part[:, c] + dot(v_ref[:, c], suffix, 1, 1)).astype(BF16)
        gv_ref[:, c] = (gv_part[:, c] + dot(k_ref[:, c], suffix, 1, 0)).astype(BF16)

    heads_loop(finish)
    store_gk = pltpu.make_async_copy(gk_ref, gk_hbm.at[0], store_sem.at[2])
    store_gv = pltpu.make_async_copy(gv_ref, gv_hbm.at[0], store_sem.at[3])
    store_gk.start()
    store_gv.start()

    third = gain_copy(gain_r3.at[others], gain_r3.at[others], 2, "dp", lax.rem(dp + 1, n_dp))
    third.wait_recv()
    for h in range(HEADS):
        gain_out[h : h + 1, :] = gain_r3[h]
    store_gain = pltpu.make_async_copy(gain_out, gg_hbm, store_sem.at[4])
    store_gain.start()

    descriptor(send_a, recv_a, 0).wait_send()
    descriptor(send_b, recv_b, 1).wait_send()
    descriptor(send_c, recv_c, 2).wait_send()
    descriptor(send_d, recv_d, 3).wait_send()
    first.wait_send()
    second.wait_send()
    third.wait_send()
    for store in (store_out, store_gq, store_gk, store_gv, store_gain):
        store.wait()


def solution(mesh):
    n_seq = mesh.shape["seq"]
    n_dp = mesh.shape["dp"]

    def per_device(queries, keys, values, gain, cotangent):
        _, tokens, features = queries.shape
        grows = HEADS // n_dp
        exact = pltpu.VMEM((tokens, features), F32)
        half = pltpu.VMEM((tokens, features), BF16)
        states = pltpu.VMEM((features, HEAD), BF16)
        big = jax.ShapeDtypeStruct(queries.shape, BF16)
        anywhere = pl.BlockSpec(memory_space=pl.ANY)
        results = pl.pallas_call(
            functools.partial(kernel, n_seq, n_dp),
            out_shape=(big, big, big, big, jax.ShapeDtypeStruct((HEADS, HEAD), F32)),
            in_specs=[anywhere] * 5,
            out_specs=(anywhere,) * 5,
            scratch_shapes=[
                half,
                half,
                half,
                half,
                pltpu.VMEM((HEADS, HEAD), F32),
                exact,
                pltpu.VMEM((features, tokens), BF16),
                half,
                exact,
                exact,
                half,
                half,
                half,
                half,
            ]
            + [states] * 8
            + [
                pltpu.VMEM((HEADS, 1, HEAD), F32),
                pltpu.VMEM((HEADS, 1, HEAD), F32),
                pltpu.VMEM((grows, 1, HEAD), F32),
                pltpu.VMEM((n_seq * grows, 1, HEAD), F32),
                pltpu.VMEM((HEADS, 1, HEAD), F32),
                pltpu.VMEM((HEADS, HEAD), F32),
                pltpu.SemaphoreType.DMA((5,)),
                pltpu.SemaphoreType.DMA((5,)),
                pltpu.SemaphoreType.DMA((4,)),
                pltpu.SemaphoreType.DMA((4,)),
                pltpu.SemaphoreType.DMA((3,)),
                pltpu.SemaphoreType.DMA((3,)),
                pltpu.SemaphoreType.DMA((4,)),
            ],
            compiler_params=pltpu.CompilerParams(collective_id=0, has_side_effects=True),
        )(queries, keys, values, gain.reshape(HEADS, HEAD), cotangent)
        return (*results[:4], results[4].reshape(features))

    sharded = P("dp", "seq", None)
    return jax.shard_map(
        per_device,
        mesh=mesh,
        in_specs=(sharded, sharded, sharded, P(), sharded),
        out_specs=(sharded, sharded, sharded, sharded, P()),
        check_vma=False,
    )
```

time: 254 us -> 82.4 us (0.32)
  blocking collectives: 138 us -> 0 us
  Pallas kernels: 0 us -> 75.7 us
  waiting for transfers between devices: 31.1 us -> 0 us
  starting transfers between devices: 24.8 us -> 0 us
  local copies, waits for them, and re-layouts: 26.8 us -> 5.8 us
  matrix products: 15.8 us -> 0 us
  other arithmetic: 15.3 us -> 0 us
    psum x1 -> x0, blocking collectives: 99.2 us -> none  [per_device(): total_gain = lax.psum(partial_gain, ('dp', 'seq'))]
    pallas_call x0 -> x1, Pallas kernels: none -> 75.7 us  [per_device(): pl.pallas_call(functools.partial(kernel, n_seq, n_dp), out_shape=(big, bi...]
    all_to_all x1 -> x0, blocking collectives: 38.4 us -> none  [prefix_swapped(): lax.all_to_all(flat_state, 'seq', split_axis=1, concat_axis=0, tiled=True)]
    all_to_all x3 -> x0, waiting for transfers between devices: 31.1 us -> none  [the longest x1 21.5 us: prefix_swapped(): lax.all_to_all(flat_state, 'seq', split_axis=1, concat_axis=0, tiled=True)]
    all_to_all x3 -> x0, starting transfers between devices: 24.8 us -> none  [the longest x2 16.7 us: prefix_swapped(): lax.all_to_all(summed_half, 'seq', split_axis=0, concat_axis=1, tiled=True)]
    dot_general x14 -> x0, matrix products: 15.8 us -> none  [the longest x2 4.52 us: prefix_swapped(): jnp.dot(triangle.astype(jnp.float32), columns, precision=lax.Precision.HI...]
    all_to_all x4 -> x0, other arithmetic: 11.6 us -> none  [prefix_swapped(): lax.all_to_all(summed_half, 'seq', split_axis=0, concat_axis=1, tiled=True)]
    unnamed x42 -> x13, local copies, waits for them, and re-layouts: 16.5 us -> 5.8 us
  transfers between devices with their start and end apart: 3 -> 0, of which waited for: 2 -> 0; matrix products, arithmetic and copies ran while one was open for 5% -> 0% of each run, Pallas kernels for 0% -> 0%
where the time goes in v1:
time: 82.4 us; the launch traced here: 82.1 us
  Pallas kernels  75.7 us (92%)
  local copies, waits for them, and re-layouts  5.8 us (7%)
    pallas_call x1, Pallas kernels, per_device(): pl.pallas_call(functools.partial(kernel, n_seq, n_dp), out_shape=(big, bi...  75.7 us
    unnamed x13, local copies, waits for them, and re-layouts  5.8 us

profile of v1, /device:TPU:1, one launch (start us, length us, event | category | flops | bytes accessed | tf_op | source)
XLA Modules:
  0.0 82.1 jit_solution(13489623732219231788)
XLA Ops:
  0.6 75.7 %shard_map.92 = (bf16[1,128,2048]{2,1,0:T(8,128)(2,1)}, bf16[1,128,2048]{2,1,0:T(8,128)(2,1)}, bf16[1,128,2048]{2,1,0:T(8,128)(2,1)}, bf16[1,128,2048]{2,1,0:T(8,128)(2,1)}, f32[16,128]{1,0:T(8,128)}) custom-call(bf16[1,128,2048]{2,1,0:T(8,128)(2,1)} %q_hbm.1, bf16[1,128,2048]{2,1,0:T(8,128)(2,1)} %k_hbm.1, bf16[1,128,2048]{2,1,0:T(8,128)(2,1)} %v_hbm.1, ...), custom_call_target="tpu_custom_call" | custom-call | tf_op jit(solution)/shard_map/pallas_call | solution.py:342
  76.3 0.0 copy-start.2
  76.3 1.9 %copy.15 = bf16[1,128,2048]{2,1,0:T(8,128)(2,1)} copy(bf16[1,128,2048]{2,1,0:T(8,128)(2,1)} %get-tuple-element.20) | data formatting | bytes 1048576
  78.3 0.0 copy-done.2
  78.3 0.0 copy-start.1
  78.3 0.8 copy.16
  79.1 0.4 copy-done.1
  79.5 0.0 copy-start
  79.5 0.8 copy.17
  80.3 0.4 copy-done
  80.7 0.0 copy-start.3
  80.7 0.8 copy.18
  81.5 0.0 copy-done.3
  81.5 0.6 copy.19
Async XLA Ops:
  76.3 2.0 %copy-start.2 = (bf16[1,128,2048]{2,1,0:T(8,128)(2,1)S(1)}, bf16[1,128,2048]{2,1,0:T(8,128)(2,1)}, u32[]{:S(2)}) copy-start(bf16[1,128,2048]{2,1,0:T(8,128)(2,1)} %get-tuple-element.21) | copy-start | bytes 1572868
  78.3 1.2 %copy-start.1 = (bf16[1,128,2048]{2,1,0:T(8,128)(2,1)S(1)}, bf16[1,128,2048]{2,1,0:T(8,128)(2,1)}, u32[]{:S(2)}) copy-start(bf16[1,128,2048]{2,1,0:T(8,128)(2,1)} %get-tuple-element.22) | copy-start | bytes 1572868
  79.5 1.2 %copy-start = (bf16[1,128,2048]{2,1,0:T(8,128)(2,1)S(1)}, bf16[1,128,2048]{2,1,0:T(8,128)(2,1)}, u32[]{:S(2)}) copy-start(bf16[1,128,2048]{2,1,0:T(8,128)(2,1)} %get-tuple-element.23) | copy-start | bytes 1572868
  80.7 0.8 copy-start.3

commit v2 on v1

v2 whole, which is shorter than its diff:
```python
import functools

import jax
import jax.numpy as jnp
from jax import lax
from jax.experimental import pallas as pl
from jax.experimental.pallas import tpu as pltpu
from jax.sharding import PartitionSpec as P

HEADS = 16
HEAD = 128
EPSILON = 1e-06
RING = 8
CHUNKS = 2
ENTRIES = 6
MESH = pl.DeviceIdType.MESH
F32 = jnp.float32
BF16 = jnp.bfloat16


def dot(a, b, ca, cb):
    return lax.dot_general(a, b, (((ca,), (cb,)), ((), ())), preferred_element_type=F32)


class ScanPass:
    def __init__(self, index, reverse, refs, send_sem, recv_sem, n_x):
        self.state, self.child, self.group, self.inbox, self.outbox, self.back, self.down, self.result = refs
        self.index, self.reverse, self.n_x = index, reverse, n_x
        self.send_sem, self.recv_sem = send_sem, recv_sem
        seq = lax.axis_index("seq")
        self.x, self.z = seq // RING, lax.rem(seq, RING)
        self.share = HEAD // n_x

    def ring(self, offset):
        return lax.rem(self.z + (offset + RING), RING)

    def rows(self, start, size):
        return pl.ds(pl.multiple_of(start, self.share), size)

    def head(self, c, k):
        return self.rows((c * CHUNKS + k) * HEAD, HEAD)

    def piece(self, c, k, x):
        return self.rows((c * CHUNKS + k) * HEAD + x * self.share, self.share)

    def spot(self, k, x, entry):
        return self.rows(((k * self.n_x + x) * ENTRIES + entry) * self.share, self.share)

    def tile(self, k, i, count):
        return self.rows((k * count + i) * HEAD, HEAD)

    def tile_part(self, k, i, count, x):
        return self.rows((k * count + i) * HEAD + x * self.share, self.share)

    def copy(self, src, dst, k, send, recv, x, z):
        return pltpu.make_async_remote_copy(
            src_ref=src,
            dst_ref=dst,
            send_sem=self.send_sem.at[self.index, k, send],
            recv_sem=self.recv_sem.at[self.index, k, recv],
            device_id={"seq": x * RING + z},
            device_id_type=MESH,
        )

    def taken(self, count, k, kind):
        part = pl.ds(0, count * self.share)
        return self.copy(self.state.at[part], self.result.at[part], k, kind, kind, self.x, self.ring(1))

    def inner(self):
        return jnp.logical_and(self.z >= 2, self.z <= 5)

    def clear(self):
        zero = jnp.zeros((HEAD, HEAD), BF16)
        few = jnp.zeros((self.share, HEAD), BF16)
        z = self.z

        @pl.when(z == 0)
        def _():
            for k in range(CHUNKS):
                self.child[self.tile(k, 0, 4), :] = zero

        @pl.when(z == RING - 1)
        def _():
            for k in range(CHUNKS):
                self.child[self.tile(k, 2, 4), :] = zero

        @pl.when(jnp.logical_not(self.inner()))
        def _():
            for k in range(CHUNKS):
                self.child[self.tile(k, 1, 4), :] = zero
                self.child[self.tile(k, 3, 4), :] = zero

        @pl.when(jnp.logical_not(jnp.logical_or(z == 2, z == 5)))
        def _():
            for k in range(CHUNKS):
                for x in range(self.n_x):
                    self.inbox[self.spot(k, x, 0), :] = few

    def send_far(self, k):
        z = self.z

        def hand(offset, to, slot, send):
            self.copy(
                self.state.at[self.head(self.ring(offset), k)],
                self.child.at[self.tile(k, slot, 4)],
                k,
                send,
                slot,
                self.x,
                to,
            ).start()

        pl.when(z < 4)(lambda: hand(4, z + 2, 1, 2))
        pl.when(z >= 4)(lambda: hand(4, z - 2, 3, 2))
        pl.when(z != RING - 1)(lambda: hand(3, z + 1, 0, 0))
        pl.when(z != 0)(lambda: hand(-3, z - 1, 2, 1))

    def send_near(self, k):
        z, n_x = self.z, self.n_x

        def direct(c, x, entry, kind):
            self.copy(
                self.state.at[self.piece(c, k, x)], self.inbox.at[self.spot(k, self.x, entry)], k, kind, kind, x, c
            ).start()

        for i in range(n_x):
            x = lax.rem(self.x + (i + 1), n_x)
            pl.when(z == RING - 1)(functools.partial(direct, 2, x, 0, 5))
            pl.when(z == 0)(functools.partial(direct, 5, x, 0, 5))
            direct(self.ring(1), x, 2, 4)
            direct(self.ring(-1), x, 4, 4)
            if i < n_x - 1:
                direct(z, x, 3, 4)
        self.inbox[self.spot(k, self.x, 3), :] = self.state[self.piece(z, k, self.x), :]

    def relay(self, k):
        z, n_x = self.z, self.n_x
        whole = n_x
        pl.when(z != 0)(lambda: self.taken(whole, k, 0).wait_recv())
        pl.when(z != RING - 1)(lambda: self.taken(whole, k, 2).wait_recv())

        @pl.when(self.inner())
        def _():
            self.taken(whole, k, 1).wait_recv()
            self.taken(whole, k, 3).wait_recv()

        for side in range(2):
            c = self.ring(2 - 4 * side)
            total = self.state[self.head(c, k), :].astype(F32)
            total = total + self.child[self.tile(k, 2 * side, 4), :].astype(F32)
            total = total + self.child[self.tile(k, 2 * side + 1, 4), :].astype(F32)
            self.group[self.tile(k, side, 2), :] = total.astype(BF16)
        for i in range(n_x):
            x = lax.rem(self.x + (i + 1), n_x)
            for side in range(2):
                self.copy(
                    self.group.at[self.tile_part(k, side, 2, x)],
                    self.inbox.at[self.spot(k, self.x, 1 + 4 * side)],
                    k,
                    4,
                    4,
                    x,
                    self.ring(2 - 4 * side),
                ).start()

    def own(self, k):
        z, n_x = self.z, self.n_x
        pl.when(jnp.logical_or(z == 2, z == 5))(lambda: self.taken(n_x, k, 5).wait_recv())
        self.taken(5 * n_x - 1, k, 4).wait_recv()
        first = jnp.where(z <= 3, 3 - z, jnp.where(z <= 5, 0, 11 - z))
        total = jnp.zeros((self.share, HEAD), F32)
        for i in range(n_x * ENTRIES):
            j = n_x * ENTRIES - 1 - i if self.reverse else i
            spot = self.spot(k, j // ENTRIES, lax.rem(first + j % ENTRIES, ENTRIES))
            self.outbox[spot, :] = total.astype(BF16)
            total = total + self.inbox[spot, :].astype(F32)

        def give(x, to, entry, kind):
            self.copy(
                self.outbox.at[self.spot(k, x, entry)], self.result.at[self.piece(z, k, self.x)], k, kind, kind, x, to
            ).start()

        def give_group(x, side):
            self.copy(
                self.outbox.at[self.spot(k, x, 1 + 4 * side)],
                self.back.at[self.tile_part(k, side, 2, self.x)],
                k,
                6,
                8 + side,
                x,
                self.ring(4 * side - 2),
            ).start()

        for i in range(n_x):
            x = lax.rem(self.x + (i + 1), n_x)
            give_group(x, 0)
            give_group(x, 1)
        for i in range(n_x):
            x = lax.rem(self.x + (i + 1), n_x)
            pl.when(z == 2)(functools.partial(give, x, RING - 1, 0, 7))
            pl.when(z == 5)(functools.partial(give, x, 0, 0, 7))
            give(x, self.ring(-1), 2, 6)
            give(x, self.ring(1), 4, 6)
            if i < n_x - 1:
                give(x, z, 3, 6)
        self.result[self.piece(z, k, self.x), :] = self.outbox[self.spot(k, self.x, 3), :]

    def pass_on(self, k):
        z = self.z
        for side in range(2):
            c = self.ring(2 - 4 * side)
            self.taken(self.n_x, k, 8 + side).wait_recv()
            base = self.back[self.tile(k, side, 2), :].astype(F32)
            mine = self.state[self.head(c, k), :].astype(F32)
            near = self.child[self.tile(k, 2 * side, 4), :].astype(F32)
            far = self.child[self.tile(k, 2 * side + 1, 4), :].astype(F32)
            if (side == 0) != self.reverse:
                for_far = base
                for_near = base + far
                for_mine = for_near + near
            else:
                for_mine = base
                for_near = base + mine
                for_far = for_near + near
            self.down[self.tile(k, 2 * side + 1, 4), :] = for_far.astype(BF16)
            self.down[self.tile(k, 2 * side, 4), :] = for_near.astype(BF16)
            self.result[self.head(c, k), :] = for_mine.astype(BF16)

        def hand(side, slot, to, send, recv):
            self.copy(
                self.down.at[self.tile(k, slot, 4)],
                self.result.at[self.head(self.ring(2 - 4 * side), k)],
                k,
                send,
                recv,
                self.x,
                to,
            ).start()

        @pl.when(self.inner())
        def _():
            hand(0, 1, z - 2, 10, 12)
            hand(1, 3, z + 2, 11, 12)

        pl.when(z != 0)(lambda: hand(0, 0, z - 1, 8, 10))
        pl.when(z != RING - 1)(lambda: hand(1, 2, z + 1, 9, 11))

    def arrive(self, k):
        z, n_x = self.z, self.n_x
        self.taken(3 * n_x - 1, k, 6).wait_recv()
        pl.when(jnp.logical_or(z == 0, z == RING - 1))(lambda: self.taken(n_x, k, 7).wait_recv())
        pl.when(z != RING - 1)(lambda: self.taken(n_x, k, 10).wait_recv())
        pl.when(z != 0)(lambda: self.taken(n_x, k, 11).wait_recv())
        self.taken(n_x, k, 12).wait_recv()

    def drain(self, k):
        z, n_x = self.z, self.n_x

        def sent(count, kind):
            self.taken(count, k, kind).wait_send()

        pl.when(z != RING - 1)(lambda: sent(n_x, 0))
        pl.when(z != 0)(lambda: sent(n_x, 1))
        sent(n_x, 2)
        sent(5 * n_x - 1, 4)
        pl.when(jnp.logical_or(z == 0, z == RING - 1))(lambda: sent(n_x, 5))
        sent(5 * n_x - 1, 6)
        pl.when(jnp.logical_or(z == 2, z == 5))(lambda: sent(n_x, 7))
        pl.when(z != 0)(lambda: sent(n_x, 8))
        pl.when(z != RING - 1)(lambda: sent(n_x, 9))

        @pl.when(self.inner())
        def _():
            sent(n_x, 10)
            sent(n_x, 11)


PASS_REFS = 8
KINDS = 13


def pass_scratch(n_x):
    tiles = CHUNKS * HEAD
    sizes = (
        HEADS * HEAD,
        4 * tiles,
        2 * tiles,
        ENTRIES * tiles,
        ENTRIES * tiles,
        2 * tiles,
        4 * tiles,
        HEADS * HEAD,
    )
    return [pltpu.VMEM((size, HEAD), BF16) for size in sizes]


def chunk_loop(k, body):
    @pl.loop(0, HEADS // CHUNKS // 4)
    def _(step):
        for inner in range(4):
            body((step * 4 + inner) * CHUNKS + k)


def kernel(
    n_seq,
    n_dp,
    q_hbm,
    k_hbm,
    v_hbm,
    gain_hbm,
    cot_hbm,
    out_hbm,
    gq_hbm,
    gk_hbm,
    gv_hbm,
    gg_hbm,
    q_ref,
    k_ref,
    v_ref,
    cot_ref,
    gain_ref,
    att_ref,
    score_ref,
    ga_ref,
    gk_part,
    gv_part,
    out_ref,
    gq_ref,
    gk_ref,
    gv_ref,
    *rest,
):
    ahead_refs, rest = rest[:PASS_REFS], rest[PASS_REFS:]
    behind_refs, rest = rest[:PASS_REFS], rest[PASS_REFS:]
    gain_part, gain_r1, gain_s2, gain_r2, gain_r3, gain_out, *sems = rest
    load_sem, store_sem, send_sem, recv_sem, gain_send_sem, gain_recv_sem = sems
    seq = lax.axis_index("seq")
    dp = lax.axis_index("dp")
    n_x = n_seq // RING
    ahead = ScanPass(0, False, ahead_refs, send_sem, recv_sem, n_x)
    behind = ScanPass(1, True, behind_refs, send_sem, recv_sem, n_x)
    tokens = q_ref.shape[0]
    features = HEADS * HEAD
    scaling = HEAD ** (-0.5)
    grows = HEADS // n_dp

    def cols(h):
        return pl.ds(pl.multiple_of(h * HEAD, HEAD), HEAD)

    loads = [
        pltpu.make_async_copy(k_hbm.at[0], k_ref, load_sem.at[0]),
        pltpu.make_async_copy(v_hbm.at[0], v_ref, load_sem.at[1]),
        pltpu.make_async_copy(q_hbm.at[0], q_ref, load_sem.at[2]),
        pltpu.make_async_copy(cot_hbm.at[0], cot_ref, load_sem.at[3]),
        pltpu.make_async_copy(gain_hbm, gain_ref, load_sem.at[4]),
    ]
    for load in loads:
        load.start()

    barrier = pltpu.get_barrier_semaphore()

    @pl.loop(1, n_seq)
    def _(k):
        peer = lax.rem(seq + k, n_seq)
        pl.semaphore_signal(barrier, inc=1, device_id={"seq": peer}, device_id_type=MESH)

    @pl.loop(1, n_dp)
    def _(k):
        peer = lax.rem(dp + k, n_dp)
        pl.semaphore_signal(barrier, inc=1, device_id={"dp": peer}, device_id_type=MESH)

    ahead.clear()
    behind.clear()

    position_t = lax.broadcasted_iota(jnp.int32, (tokens, tokens), 0)
    position_u = lax.broadcasted_iota(jnp.int32, (tokens, tokens), 1)
    causal = position_t >= position_u

    loads[0].wait()
    loads[1].wait()

    def state_of(h):
        c = cols(h)
        ahead.state[c, :] = dot(k_ref[:, c], v_ref[:, c], 0, 0).astype(BF16)

    chunk_loop(0, state_of)
    pl.semaphore_wait(barrier, n_seq - 1 + n_dp - 1)
    ahead.send_far(0)
    chunk_loop(1, state_of)
    ahead.send_far(1)
    ahead.send_near(0)
    ahead.send_near(1)

    loads[2].wait()
    loads[3].wait()
    loads[4].wait()

    def local_of(h):
        c = cols(h)
        raw = dot(q_ref[:, c], k_ref[:, c], 1, 1)
        score = jnp.where(causal, raw * scaling, 0.0).astype(BF16)
        score_ref[c, :] = score
        att_ref[:, c] = dot(score, v_ref[:, c], 1, 0)

    chunk_loop(0, local_of)
    ahead.relay(0)
    ahead.relay(1)
    chunk_loop(1, local_of)
    ahead.own(0)
    ahead.own(1)
    ahead.pass_on(0)
    ahead.pass_on(1)

    def attend(chunk, step, carry):
        squares, inner = carry
        for k in range(4):
            h = (step * 4 + k) * CHUNKS + chunk
            c = cols(h)
            att = att_ref[:, c] + scaling * dot(q_ref[:, c], ahead.result[c, :], 1, 0)
            att_ref[:, c] = att
            squares = squares + att * att
            inner = inner + att * (cot_ref[:, c].astype(F32) * gain_ref[pl.ds(h, 1), :])
        return squares, inner

    zero = jnp.zeros((tokens, HEAD), F32)
    carry = (zero, zero)
    for chunk in range(CHUNKS):
        ahead.arrive(chunk)
        carry = lax.fori_loop(0, HEADS // CHUNKS // 4, functools.partial(attend, chunk), carry)
    squares, inner = carry
    root = jnp.sqrt(jnp.sum(squares, axis=1, keepdims=True) / features + EPSILON)
    inverse = 1.0 / root
    mean = jnp.sum(inner, axis=1, keepdims=True) * inverse / features

    def normalize(h):
        c = cols(h)
        weight = gain_ref[pl.ds(h, 1), :]
        upstream = cot_ref[:, c].astype(F32)
        normalized = att_ref[:, c] * inverse
        out_ref[:, c] = (weight * normalized).astype(BF16)
        gain_part[h] = jnp.sum(upstream * normalized, axis=0, keepdims=True)
        grad = ((upstream * weight - normalized * mean) * inverse).astype(BF16)
        ga_ref[:, c] = grad
        behind.state[c, :] = (scaling * dot(q_ref[:, c], grad, 0, 0)).astype(BF16)

    chunk_loop(0, normalize)
    behind.send_far(0)
    chunk_loop(1, normalize)
    behind.send_far(1)
    behind.send_near(0)
    behind.send_near(1)

    def gain_copy(src, dst, index, axis, peer):
        return pltpu.make_async_remote_copy(
            src_ref=src,
            dst_ref=dst,
            send_sem=gain_send_sem.at[index],
            recv_sem=gain_recv_sem.at[index],
            device_id={axis: peer},
            device_id_type=MESH,
        )

    def part(j):
        return pl.ds(j * grows, grows)

    @pl.loop(1, n_dp)
    def _(k):
        peer = lax.rem(dp + k, n_dp)
        gain_copy(gain_part.at[part(peer)], gain_r1.at[part(dp)], 0, "dp", peer).start()

    store_out = pltpu.make_async_copy(out_ref, out_hbm.at[0], store_sem.at[0])
    store_out.start()

    def grads(h):
        c = cols(h)
        grad = ga_ref[:, c]
        gs = jnp.where(causal, dot(grad, v_ref[:, c], 1, 1), 0.0).astype(BF16)
        query = dot(gs, k_ref[:, c], 1, 0) + dot(grad, ahead.result[c, :], 1, 1)
        gq_ref[:, c] = (scaling * query).astype(BF16)
        gk_part[:, c] = scaling * dot(gs, q_ref[:, c], 0, 0)
        gv_part[:, c] = dot(score_ref[c, :], grad, 0, 0)

    chunk_loop(0, grads)
    behind.relay(0)
    behind.relay(1)
    chunk_loop(1, grads)
    store_gq = pltpu.make_async_copy(gq_ref, gq_hbm.at[0], store_sem.at[1])
    store_gq.start()

    gain_r1[part(dp)] = gain_part[part(dp)]
    others = pl.ds(0, (n_dp - 1) * grows)
    first = gain_copy(gain_part.at[others], gain_r1.at[others], 0, "dp", lax.rem(dp + 1, n_dp))
    first.wait_recv()
    summed = jnp.zeros((grows, 1, HEAD), F32)
    for j in range(n_dp):
        summed = summed + gain_r1[pl.ds(j * grows, grows)]
    gain_s2[...] = summed

    @pl.loop(1, n_seq)
    def _(k):
        peer = lax.rem(seq + k, n_seq)
        gain_copy(gain_s2, gain_r2.at[pl.ds(seq * grows, grows)], 1, "seq", peer).start()

    behind.own(0)
    behind.own(1)

    behind.pass_on(0)
    behind.pass_on(1)

    gain_r2[pl.ds(seq * grows, grows)] = summed
    some = pl.ds(0, (n_seq - 1) * grows)
    second = gain_copy(gain_r2.at[some], gain_r2.at[some], 1, "seq", lax.rem(seq + 1, n_seq))
    second.wait_recv()

    def add(j, total):
        return total + gain_r2[pl.ds(j * grows, grows)]

    total = lax.fori_loop(0, n_seq, add, jnp.zeros((grows, 1, HEAD), F32)) / n_dp
    gain_r3[part(dp)] = total

    @pl.loop(1, n_dp)
    def _(k):
        peer = lax.rem(dp + k, n_dp)
        gain_copy(gain_r3.at[part(dp)], gain_r3.at[part(dp)], 2, "dp", peer).start()


    def finish(h):
        c = cols(h)
        suffix = behind.result[c, :]
        gk_ref[:, c] = (gk_part[:, c] + dot(v_ref[:, c], suffix, 1, 1)).astype(BF16)
        gv_ref[:, c] = (gv_part[:, c] + dot(k_ref[:, c], suffix, 1, 0)).astype(BF16)

    for chunk in range(CHUNKS):
        behind.arrive(chunk)
        chunk_loop(chunk, finish)
    store_gk = pltpu.make_async_copy(gk_ref, gk_hbm.at[0], store_sem.at[2])
    store_gv = pltpu.make_async_copy(gv_ref, gv_hbm.at[0], store_sem.at[3])
    store_gk.start()
    store_gv.start()

    third = gain_copy(gain_r3.at[others], gain_r3.at[others], 2, "dp", lax.rem(dp + 1, n_dp))
    third.wait_recv()
    for h in range(HEADS):
        gain_out[h : h + 1, :] = gain_r3[h]
    store_gain = pltpu.make_async_copy(gain_out, gg_hbm, store_sem.at[4])
    store_gain.start()

    for chunk in range(CHUNKS):
        ahead.drain(chunk)
        behind.drain(chunk)
    first.wait_send()
    second.wait_send()
    third.wait_send()
    for store in (store_out, store_gq, store_gk, store_gv, store_gain):
        store.wait()


def hand_out(*refs):
    sources, targets, sem = refs[:5], refs[5:10], refs[10]
    stores = [pltpu.make_async_copy(a, b, sem.at[i]) for i, (a, b) in enumerate(zip(sources, targets))]
    for store in stores:
        store.start()
    for store in stores:
        store.wait()


def stay(array):
    return pltpu.with_memory_space_constraint(array, pltpu.HBM)


def solution(mesh):
    n_seq = mesh.shape["seq"]
    n_dp = mesh.shape["dp"]

    def per_device(queries, keys, values, gain, cotangent):
        _, tokens, features = queries.shape
        grows = HEADS // n_dp
        exact = pltpu.VMEM((tokens, features), F32)
        half = pltpu.VMEM((tokens, features), BF16)
        big = jax.ShapeDtypeStruct(queries.shape, BF16)
        anywhere = pl.BlockSpec(memory_space=pl.ANY)
        results = pl.pallas_call(
            functools.partial(kernel, n_seq, n_dp),
            out_shape=(big, big, big, big, jax.ShapeDtypeStruct((HEADS, HEAD), F32)),
            in_specs=[pl.BlockSpec(memory_space=pltpu.HBM)] * 5,
            out_specs=(anywhere,) * 5,
            scratch_shapes=[
                half,
                half,
                half,
                half,
                pltpu.VMEM((HEADS, HEAD), F32),
                exact,
                pltpu.VMEM((features, tokens), BF16),
                half,
                exact,
                exact,
                half,
                half,
                half,
                half,
            ]
            + pass_scratch(n_seq // RING) * 2
            + [
                pltpu.VMEM((HEADS, 1, HEAD), F32),
                pltpu.VMEM((HEADS, 1, HEAD), F32),
                pltpu.VMEM((grows, 1, HEAD), F32),
                pltpu.VMEM((n_seq * grows, 1, HEAD), F32),
                pltpu.VMEM((HEADS, 1, HEAD), F32),
                pltpu.VMEM((HEADS, HEAD), F32),
                pltpu.SemaphoreType.DMA((5,)),
                pltpu.SemaphoreType.DMA((5,)),
                pltpu.SemaphoreType.DMA((2, CHUNKS, KINDS)),
                pltpu.SemaphoreType.DMA((2, CHUNKS, KINDS)),
                pltpu.SemaphoreType.DMA((3,)),
                pltpu.SemaphoreType.DMA((3,)),
            ],
            compiler_params=pltpu.CompilerParams(
                collective_id=0, has_side_effects=True, vmem_limit_bytes=32 * 2**20
            ),
        )(*(stay(a) for a in (queries, keys, values, gain.reshape(HEADS, HEAD), cotangent)))
        small = jax.ShapeDtypeStruct((HEADS, HEAD), F32)
        results = pl.pallas_call(
            hand_out,
            out_shape=(big, big, big, big, small),
            in_specs=[anywhere] * 5,
            out_specs=(anywhere,) * 5,
            scratch_shapes=[pltpu.SemaphoreType.DMA((5,))],
            compiler_params=pltpu.CompilerParams(vmem_limit_bytes=2**20),
        )(*results)
        return (*results[:4], results[4].reshape(features))

    sharded = P("dp", "seq", None)
    return jax.shard_map(
        per_device,
        mesh=mesh,
        in_specs=(sharded, sharded, sharded, P(), sharded),
        out_specs=(sharded, sharded, sharded, sharded, P()),
        check_vma=False,
    )
```

time: 82.4 us -> 67.7 us (0.82)
  Pallas kernels: 75.7 us -> 67 us
  local copies, waits for them, and re-layouts: 5.8 us -> 0 us
    pallas_call x1, Pallas kernels: 75.7 us -> 65.6 us  [per_device(): pl.pallas_call(functools.partial(kernel, n_seq, n_dp), out_shape=(big, bi...]
    unnamed x13 -> x0, local copies, waits for them, and re-layouts: 5.8 us -> none
    pallas_call x0 -> x1, Pallas kernels: none -> 1.36 us  [per_device(): pl.pallas_call(hand_out, out_shape=(big, big, big, big, small), in_specs=...]
where the time goes in v2:
time: 67.7 us; the launch traced here: 67.6 us
  Pallas kernels  67 us (99%)
    pallas_call x1, Pallas kernels, per_device(): pl.pallas_call(functools.partial(kernel, n_seq, n_dp), out_shape=(big, bi...  65.6 us
    pallas_call x1, Pallas kernels, per_device(): pl.pallas_call(hand_out, out_shape=(big, big, big, big, small), in_specs=...  1.36 us

profile of v2, /device:TPU:1, one launch (start us, length us, event | category | flops | bytes accessed | tf_op | source)
XLA Modules:
  0.0 67.6 jit_solution(1884234383556172809)
XLA Ops:
  0.6 65.6 %shard_map.92 = (bf16[1,128,2048]{2,1,0:T(8,128)(2,1)S(1)}, bf16[1,128,2048]{2,1,0:T(8,128)(2,1)S(1)}, bf16[1,128,2048]{2,1,0:T(8,128)(2,1)S(1)}, bf16[1,128,2048]{2,1,0:T(8,128)(2,1)S(1)}, f32[16,128]{1,0:T(8,128)S(1)}) custom-call(bf16[1,128,2048]{2,1,0:T(8,128)(2,1)} %q_hbm.1, bf16[1,128,2048]{2,1,0:T(8,128)(2,1)} %k_hbm.1, bf16[1,128,2048]{2,1,0:T(8,128)(2,1)} %v_hbm.1, ...), custom_call_target="tpu_custom_call" | custom-call | tf_op jit(solution)/shard_map/pallas_call | solution.py:582
  66.2 1.4 %shard_map.93 = (bf16[1,128,2048]{2,1,0:T(8,128)(2,1)}, bf16[1,128,2048]{2,1,0:T(8,128)(2,1)}, bf16[1,128,2048]{2,1,0:T(8,128)(2,1)}, bf16[1,128,2048]{2,1,0:T(8,128)(2,1)}, f32[16,128]{1,0:T(8,128)}) custom-call(bf16[1,128,2048]{2,1,0:T(8,128)(2,1)S(1)} %get-tuple-element.15.refs_0_, bf16[1,128,2048]{2,1,0:T(8,128)(2,1)S(1)} %get-tuple-element.16.refs_1_, ...), custom_call_target="tpu_custom_call" | custom-call | tf_op jit(solution)/shard_map/pallas_call | solution.py:623

commit v3 on v2

--- a/solution.py
+++ b/solution.py
@@ -66,31 +66,35 @@
         part = pl.ds(0, count * self.share)
         return self.copy(self.state.at[part], self.result.at[part], k, kind, kind, self.x, self.ring(1))
 
-    def inner(self):
-        return jnp.logical_and(self.z >= 2, self.z <= 5)
+    def odd(self):
+        return jnp.logical_or(self.z == 0, self.z == RING - 1)
+
+    def even_inner(self):
+        return jnp.logical_and(self.z != 0, lax.rem(self.z, 2) == 0)
+
+    def odd_inner(self):
+        return jnp.logical_and(self.z != RING - 1, lax.rem(self.z, 2) == 1)
+
+    def odd_owner(self):
+        return jnp.logical_or(self.z == 2, self.z == 5)
+
+    def odd_target(self):
+        return jnp.where(self.z == 0, 5, 2)
 
     def clear(self):
         zero = jnp.zeros((HEAD, HEAD), BF16)
         few = jnp.zeros((self.share, HEAD), BF16)
-        z = self.z
-
-        @pl.when(z == 0)
-        def _():
+
+        def blank(slot):
             for k in range(CHUNKS):
-                self.child[self.tile(k, 0, 4), :] = zero
-
-        @pl.when(z == RING - 1)
-        def _():
-            for k in range(CHUNKS):
-                self.child[self.tile(k, 2, 4), :] = zero
-
-        @pl.when(jnp.logical_not(self.inner()))
-        def _():
-            for k in range(CHUNKS):
-                self.child[self.tile(k, 1, 4), :] = zero
-                self.child[self.tile(k, 3, 4), :] = zero
-
-        @pl.when(jnp.logical_not(jnp.logical_or(z == 2, z == 5)))
+                self.child[self.tile(k, slot, 5), :] = zero
+
+        pl.when(self.z == 0)(lambda: blank(0))
+        pl.when(self.z == RING - 1)(lambda: blank(2))
+        pl.when(jnp.logical_not(self.even_inner()))(lambda: blank(1))
+        pl.when(jnp.logical_not(self.odd_inner()))(lambda: blank(3))
+
+        @pl.when(jnp.logical_not(self.odd_owner()))
         def _():
             for k in range(CHUNKS):
                 for x in range(self.n_x):
@@ -102,16 +106,19 @@
         def hand(offset, to, slot, send):
             self.copy(
                 self.state.at[self.head(self.ring(offset), k)],
-                self.child.at[self.tile(k, slot, 4)],
+                self.child.at[self.tile(k, slot, 5)],
                 k,
                 send,
-                slot,
+                slot if slot < 4 else 13,
                 self.x,
                 to,
             ).start()
 
-        pl.when(z < 4)(lambda: hand(4, z + 2, 1, 2))
-        pl.when(z >= 4)(lambda: hand(4, z - 2, 3, 2))
+        even = lax.rem(z, 2) == 0
+        pl.when(jnp.logical_and(even, z != 6))(lambda: hand(4, z + 2, 1, 2))
+        pl.when(jnp.logical_not(jnp.logical_or(even, z == 1)))(lambda: hand(4, z - 2, 3, 2))
+        pl.when(z == 6)(lambda: hand(4, z + 1, 4, 2))
+        pl.when(z == 1)(lambda: hand(4, z - 1, 4, 2))
         pl.when(z != RING - 1)(lambda: hand(3, z + 1, 0, 0))
         pl.when(z != 0)(lambda: hand(-3, z - 1, 2, 1))
 
@@ -125,8 +132,6 @@
 
         for i in range(n_x):
             x = lax.rem(self.x + (i + 1), n_x)
-            pl.when(z == RING - 1)(functools.partial(direct, 2, x, 0, 5))
-            pl.when(z == 0)(functools.partial(direct, 5, x, 0, 5))
             direct(self.ring(1), x, 2, 4)
             direct(self.ring(-1), x, 4, 4)
             if i < n_x - 1:
@@ -136,36 +141,44 @@
     def relay(self, k):
         z, n_x = self.z, self.n_x
         whole = n_x
-        pl.when(z != 0)(lambda: self.taken(whole, k, 0).wait_recv())
-        pl.when(z != RING - 1)(lambda: self.taken(whole, k, 2).wait_recv())
-
-        @pl.when(self.inner())
-        def _():
-            self.taken(whole, k, 1).wait_recv()
-            self.taken(whole, k, 3).wait_recv()
-
         for side in range(2):
+            if side == 0:
+                pl.when(z != 0)(lambda: self.taken(whole, k, 0).wait_recv())
+                pl.when(self.even_inner())(lambda: self.taken(whole, k, 1).wait_recv())
+            else:
+                pl.when(z != RING - 1)(lambda: self.taken(whole, k, 2).wait_recv())
+                pl.when(self.odd_inner())(lambda: self.taken(whole, k, 3).wait_recv())
             c = self.ring(2 - 4 * side)
             total = self.state[self.head(c, k), :].astype(F32)
-            total = total + self.child[self.tile(k, 2 * side, 4), :].astype(F32)
-            total = total + self.child[self.tile(k, 2 * side + 1, 4), :].astype(F32)
-            self.group[self.tile(k, side, 2), :] = total.astype(BF16)
-        for i in range(n_x):
-            x = lax.rem(self.x + (i + 1), n_x)
-            for side in range(2):
+            total = total + self.child[self.tile(k, 2 * side, 5), :].astype(F32)
+            total = total + self.child[self.tile(k, 2 * side + 1, 5), :].astype(F32)
+            self.group[self.tile(k, side, 3), :] = total.astype(BF16)
+            for i in range(n_x):
+                x = lax.rem(self.x + (i + 1), n_x)
                 self.copy(
-                    self.group.at[self.tile_part(k, side, 2, x)],
+                    self.group.at[self.tile_part(k, side, 3, x)],
                     self.inbox.at[self.spot(k, self.x, 1 + 4 * side)],
                     k,
                     4,
                     4,
                     x,
-                    self.ring(2 - 4 * side),
+                    c,
                 ).start()
+
+        @pl.when(self.odd())
+        def _():
+            self.taken(whole, k, 13).wait_recv()
+            c = self.odd_target()
+            total = self.state[self.head(c, k), :].astype(F32) + self.child[self.tile(k, 4, 5), :].astype(F32)
+            self.group[self.tile(k, 2, 3), :] = total.astype(BF16)
+            for i in range(n_x):
+                x = lax.rem(self.x + (i + 1), n_x)
+                source = self.group.at[self.tile_part(k, 2, 3, x)]
+                self.copy(source, self.inbox.at[self.spot(k, self.x, 0)], k, 5, 5, x, c).start()
 
     def own(self, k):
         z, n_x = self.z, self.n_x
-        pl.when(jnp.logical_or(z == 2, z == 5))(lambda: self.taken(n_x, k, 5).wait_recv())
+        pl.when(self.odd_owner())(lambda: self.taken(n_x, k, 5).wait_recv())
         self.taken(5 * n_x - 1, k, 4).wait_recv()
         first = jnp.where(z <= 3, 3 - z, jnp.where(z <= 5, 0, 11 - z))
         total = jnp.zeros((self.share, HEAD), F32)
@@ -175,15 +188,10 @@
             self.outbox[spot, :] = total.astype(BF16)
             total = total + self.inbox[spot, :].astype(F32)
 
-        def give(x, to, entry, kind):
-            self.copy(
-                self.outbox.at[self.spot(k, x, entry)], self.result.at[self.piece(z, k, self.x)], k, kind, kind, x, to
-            ).start()
-
         def give_group(x, side):
             self.copy(
                 self.outbox.at[self.spot(k, x, 1 + 4 * side)],
-                self.back.at[self.tile_part(k, side, 2, self.x)],
+                self.back.at[self.tile_part(k, side, 3, self.x)],
                 k,
                 6,
                 8 + side,
@@ -195,10 +203,25 @@
             x = lax.rem(self.x + (i + 1), n_x)
             give_group(x, 0)
             give_group(x, 1)
+
+        @pl.when(self.odd_owner())
+        def _():
+            for i in range(n_x):
+                x = lax.rem(self.x + (i + 1), n_x)
+                target = self.back.at[self.tile_part(k, 2, 3, self.x)]
+                to = jnp.where(z == 2, RING - 1, 0)
+                self.copy(self.outbox.at[self.spot(k, x, 0)], target, k, 7, 7, x, to).start()
+
+    def give_near(self, k):
+        z, n_x = self.z, self.n_x
+
+        def give(x, to, entry, kind):
+            self.copy(
+                self.outbox.at[self.spot(k, x, entry)], self.result.at[self.piece(z, k, self.x)], k, kind, kind, x, to
+            ).start()
+
         for i in range(n_x):
             x = lax.rem(self.x + (i + 1), n_x)
-            pl.when(z == 2)(functools.partial(give, x, RING - 1, 0, 7))
-            pl.when(z == 5)(functools.partial(give, x, 0, 0, 7))
             give(x, self.ring(-1), 2, 6)
             give(x, self.ring(1), 4, 6)
             if i < n_x - 1:
@@ -210,10 +233,10 @@
         for side in range(2):
             c = self.ring(2 - 4 * side)
             self.taken(self.n_x, k, 8 + side).wait_recv()
-            base = self.back[self.tile(k, side, 2), :].astype(F32)
+            base = self.back[self.tile(k, side, 3), :].astype(F32)
             mine = self.state[self.head(c, k), :].astype(F32)
-            near = self.child[self.tile(k, 2 * side, 4), :].astype(F32)
-            far = self.child[self.tile(k, 2 * side + 1, 4), :].astype(F32)
+            near = self.child[self.tile(k, 2 * side, 5), :].astype(F32)
+            far = self.child[self.tile(k, 2 * side + 1, 5), :].astype(F32)
             if (side == 0) != self.reverse:
                 for_far = base
                 for_near = base + far
@@ -222,13 +245,13 @@
                 for_mine = base
                 for_near = base + mine
                 for_far = for_near + near
-            self.down[self.tile(k, 2 * side + 1, 4), :] = for_far.astype(BF16)
-            self.down[self.tile(k, 2 * side, 4), :] = for_near.astype(BF16)
+            self.down[self.tile(k, 2 * side + 1, 5), :] = for_far.astype(BF16)
+            self.down[self.tile(k, 2 * side, 5), :] = for_near.astype(BF16)
             self.result[self.head(c, k), :] = for_mine.astype(BF16)
 
         def hand(side, slot, to, send, recv):
             self.copy(
-                self.down.at[self.tile(k, slot, 4)],
+                self.down.at[self.tile(k, slot, 5)],
                 self.result.at[self.head(self.ring(2 - 4 * side), k)],
                 k,
                 send,
@@ -237,18 +260,29 @@
                 to,
             ).start()
 
-        @pl.when(self.inner())
-        def _():
-            hand(0, 1, z - 2, 10, 12)
-            hand(1, 3, z + 2, 11, 12)
-
+        pl.when(self.even_inner())(lambda: hand(0, 1, z - 2, 10, 12))
+        pl.when(self.odd_inner())(lambda: hand(1, 3, z + 2, 10, 12))
         pl.when(z != 0)(lambda: hand(0, 0, z - 1, 8, 10))
         pl.when(z != RING - 1)(lambda: hand(1, 2, z + 1, 9, 11))
+
+        @pl.when(self.odd())
+        def _():
+            self.taken(self.n_x, k, 7).wait_recv()
+            c = self.odd_target()
+            base = self.back[self.tile(k, 2, 3), :].astype(F32)
+            mine = base + self.child[self.tile(k, 4, 5), :].astype(F32)
+            theirs = base + self.state[self.head(c, k), :].astype(F32)
+            their_turn = (z == RING - 1) != self.reverse
+            self.down[self.tile(k, 4, 5), :] = jnp.where(their_turn, base, theirs).astype(BF16)
+            self.result[self.head(c, k), :] = jnp.where(their_turn, mine, base).astype(BF16)
+            to = jnp.where(z == 0, 1, RING - 2)
+            self.copy(
+                self.down.at[self.tile(k, 4, 5)], self.result.at[self.head(c, k)], k, 10, 12, self.x, to
+            ).start()
 
     def arrive(self, k):
         z, n_x = self.z, self.n_x
         self.taken(3 * n_x - 1, k, 6).wait_recv()
-        pl.when(jnp.logical_or(z == 0, z == RING - 1))(lambda: self.taken(n_x, k, 7).wait_recv())
         pl.when(z != RING - 1)(lambda: self.taken(n_x, k, 10).wait_recv())
         pl.when(z != 0)(lambda: self.taken(n_x, k, 11).wait_recv())
         self.taken(n_x, k, 12).wait_recv()
@@ -263,32 +297,28 @@
         pl.when(z != 0)(lambda: sent(n_x, 1))
         sent(n_x, 2)
         sent(5 * n_x - 1, 4)
-        pl.when(jnp.logical_or(z == 0, z == RING - 1))(lambda: sent(n_x, 5))
+        pl.when(self.odd())(lambda: sent(n_x, 5))
         sent(5 * n_x - 1, 6)
-        pl.when(jnp.logical_or(z == 2, z == 5))(lambda: sent(n_x, 7))
+        pl.when(self.odd_owner())(lambda: sent(n_x, 7))
         pl.when(z != 0)(lambda: sent(n_x, 8))
         pl.when(z != RING - 1)(lambda: sent(n_x, 9))
-
-        @pl.when(self.inner())
-        def _():
-            sent(n_x, 10)
-            sent(n_x, 11)
+        sent(n_x, 10)
 
 
 PASS_REFS = 8
-KINDS = 13
+KINDS = 14
 
 
 def pass_scratch(n_x):
     tiles = CHUNKS * HEAD
     sizes = (
         HEADS * HEAD,
-        4 * tiles,
-        2 * tiles,
+        5 * tiles,
+        3 * tiles,
         ENTRIES * tiles,
         ENTRIES * tiles,
-        2 * tiles,
-        4 * tiles,
+        3 * tiles,
+        5 * tiles,
         HEADS * HEAD,
     )
     return [pltpu.VMEM((size, HEAD), BF16) for size in sizes]
@@ -408,6 +438,8 @@
     chunk_loop(1, local_of)
     ahead.own(0)
     ahead.own(1)
+    ahead.give_near(0)
+    ahead.give_near(1)
     ahead.pass_on(0)
     ahead.pass_on(1)
 
@@ -503,6 +535,8 @@
 
     behind.own(0)
     behind.own(1)
+    behind.give_near(0)
+    behind.give_near(1)
 
     behind.pass_on(0)
     behind.pass_on(1)

time: 67.7 us -> 66.4 us (0.981)
  Pallas kernels: 67 us -> 65.6 us
    pallas_call x1, Pallas kernels: 65.6 us -> 64.3 us  [per_device(): pl.pallas_call(functools.partial(kernel, n_seq, n_dp), out_shape=(big, bi...]
where the time goes in v3:
time: 66.4 us; the launch traced here: 66.3 us
  Pallas kernels  65.6 us (99%)
    pallas_call x1, Pallas kernels, per_device(): pl.pallas_call(functools.partial(kernel, n_seq, n_dp), out_shape=(big, bi...  64.3 us
    pallas_call x1, Pallas kernels, per_device(): pl.pallas_call(hand_out, out_shape=(big, big, big, big, small), in_specs=...  1.36 us

profile of v3, /device:TPU:1, one launch (start us, length us, event | category | flops | bytes accessed | tf_op | source)
XLA Modules:
  0.0 66.3 jit_solution(11421664276366356458)
XLA Ops:
  0.6 64.3 %shard_map.92 = (bf16[1,128,2048]{2,1,0:T(8,128)(2,1)S(1)}, bf16[1,128,2048]{2,1,0:T(8,128)(2,1)S(1)}, bf16[1,128,2048]{2,1,0:T(8,128)(2,1)S(1)}, bf16[1,128,2048]{2,1,0:T(8,128)(2,1)S(1)}, f32[16,128]{1,0:T(8,128)S(1)}) custom-call(bf16[1,128,2048]{2,1,0:T(8,128)(2,1)} %q_hbm.1, bf16[1,128,2048]{2,1,0:T(8,128)(2,1)} %k_hbm.1, bf16[1,128,2048]{2,1,0:T(8,128)(2,1)} %v_hbm.1, ...), custom_call_target="tpu_custom_call" | custom-call | tf_op jit(solution)/shard_map/pallas_call | solution.py:616
  64.9 1.4 %shard_map.93 = (bf16[1,128,2048]{2,1,0:T(8,128)(2,1)}, bf16[1,128,2048]{2,1,0:T(8,128)(2,1)}, bf16[1,128,2048]{2,1,0:T(8,128)(2,1)}, bf16[1,128,2048]{2,1,0:T(8,128)(2,1)}, f32[16,128]{1,0:T(8,128)}) custom-call(bf16[1,128,2048]{2,1,0:T(8,128)(2,1)S(1)} %get-tuple-element.15.refs_0_, bf16[1,128,2048]{2,1,0:T(8,128)(2,1)S(1)} %get-tuple-element.16.refs_1_, ...), custom_call_target="tpu_custom_call" | custom-call | tf_op jit(solution)/shard_map/pallas_call | solution.py:657

commit v4 on v3

--- a/solution.py
+++ b/solution.py
@@ -38,10 +38,10 @@
         return pl.ds(pl.multiple_of(start, self.share), size)
 
     def head(self, c, k):
-        return self.rows((c * CHUNKS + k) * HEAD, HEAD)
+        return self.rows((k * RING + c) * HEAD, HEAD)
 
     def piece(self, c, k, x):
-        return self.rows((c * CHUNKS + k) * HEAD + x * self.share, self.share)
+        return self.rows((k * RING + c) * HEAD + x * self.share, self.share)
 
     def spot(self, k, x, entry):
         return self.rows(((k * self.n_x + x) * ENTRIES + entry) * self.share, self.share)
@@ -325,10 +325,10 @@
 
 
 def chunk_loop(k, body):
-    @pl.loop(0, HEADS // CHUNKS // 4)
+    @pl.loop(0, RING // 4)
     def _(step):
         for inner in range(4):
-            body((step * 4 + inner) * CHUNKS + k)
+            body(k * RING + step * 4 + inner)
 
 
 def kernel(
@@ -362,7 +362,7 @@
 ):
     ahead_refs, rest = rest[:PASS_REFS], rest[PASS_REFS:]
     behind_refs, rest = rest[:PASS_REFS], rest[PASS_REFS:]
-    gain_part, gain_r1, gain_s2, gain_r2, gain_r3, gain_out, *sems = rest
+    gain_part, gain_r1, gain_s2, gain_r2, gain_s3, gain_r3, gain_r4, gain_out, *sems = rest
     load_sem, store_sem, send_sem, recv_sem, gain_send_sem, gain_recv_sem = sems
     seq = lax.axis_index("seq")
     dp = lax.axis_index("dp")
@@ -372,27 +372,35 @@
     tokens = q_ref.shape[0]
     features = HEADS * HEAD
     scaling = HEAD ** (-0.5)
-    grows = HEADS // n_dp
+    grows = HEADS // n_x
 
     def cols(h):
         return pl.ds(pl.multiple_of(h * HEAD, HEAD), HEAD)
 
+    half = features // CHUNKS
+    early = []
+    for k in range(CHUNKS):
+        for i, (src, dst) in enumerate(((k_hbm, k_ref), (v_hbm, v_ref))):
+            part_of = pl.ds(k * half, half)
+            early.append(
+                pltpu.make_async_copy(src.at[0, :, part_of], dst.at[:, part_of], load_sem.at[CHUNKS * k + i])
+            )
     loads = [
-        pltpu.make_async_copy(k_hbm.at[0], k_ref, load_sem.at[0]),
-        pltpu.make_async_copy(v_hbm.at[0], v_ref, load_sem.at[1]),
-        pltpu.make_async_copy(q_hbm.at[0], q_ref, load_sem.at[2]),
-        pltpu.make_async_copy(cot_hbm.at[0], cot_ref, load_sem.at[3]),
-        pltpu.make_async_copy(gain_hbm, gain_ref, load_sem.at[4]),
+        pltpu.make_async_copy(q_hbm.at[0], q_ref, load_sem.at[4]),
+        pltpu.make_async_copy(cot_hbm.at[0], cot_ref, load_sem.at[5]),
+        pltpu.make_async_copy(gain_hbm, gain_ref, load_sem.at[6]),
     ]
-    for load in loads:
+    for load in early + loads:
         load.start()
 
     barrier = pltpu.get_barrier_semaphore()
 
-    @pl.loop(1, n_seq)
-    def _(k):
-        peer = lax.rem(seq + k, n_seq)
-        pl.semaphore_signal(barrier, inc=1, device_id={"seq": peer}, device_id_type=MESH)
+    for step in range(n_x):
+        for offset in (1, -1, 2, -2, 0, 3, -3, 4):
+            if step == 0 and offset == 0:
+                continue
+            peer = lax.rem(ahead.x + step, n_x) * RING + ahead.ring(offset)
+            pl.semaphore_signal(barrier, inc=1, device_id={"seq": peer}, device_id_type=MESH)
 
     @pl.loop(1, n_dp)
     def _(k):
@@ -406,24 +414,24 @@
     position_u = lax.broadcasted_iota(jnp.int32, (tokens, tokens), 1)
     causal = position_t >= position_u
 
-    loads[0].wait()
-    loads[1].wait()
-
     def state_of(h):
         c = cols(h)
         ahead.state[c, :] = dot(k_ref[:, c], v_ref[:, c], 0, 0).astype(BF16)
 
+    early[0].wait()
+    early[1].wait()
     chunk_loop(0, state_of)
     pl.semaphore_wait(barrier, n_seq - 1 + n_dp - 1)
     ahead.send_far(0)
+    early[2].wait()
+    early[3].wait()
     chunk_loop(1, state_of)
     ahead.send_far(1)
     ahead.send_near(0)
     ahead.send_near(1)
 
-    loads[2].wait()
-    loads[3].wait()
-    loads[4].wait()
+    for load in loads:
+        load.wait()
 
     def local_of(h):
         c = cols(h)
@@ -446,7 +454,7 @@
     def attend(chunk, step, carry):
         squares, inner = carry
         for k in range(4):
-            h = (step * 4 + k) * CHUNKS + chunk
+            h = chunk * RING + step * 4 + k
             c = cols(h)
             att = att_ref[:, c] + scaling * dot(q_ref[:, c], ahead.result[c, :], 1, 0)
             att_ref[:, c] = att
@@ -458,29 +466,30 @@
     carry = (zero, zero)
     for chunk in range(CHUNKS):
         ahead.arrive(chunk)
-        carry = lax.fori_loop(0, HEADS // CHUNKS // 4, functools.partial(attend, chunk), carry)
+        carry = lax.fori_loop(0, RING // 4, functools.partial(attend, chunk), carry)
     squares, inner = carry
     root = jnp.sqrt(jnp.sum(squares, axis=1, keepdims=True) / features + EPSILON)
     inverse = 1.0 / root
     mean = jnp.sum(inner, axis=1, keepdims=True) * inverse / features
 
+    def pull(h):
+        c = cols(h)
+        upstream = cot_ref[:, c].astype(F32)
+        normalized = att_ref[:, c] * inverse
+        grad = ((upstream * gain_ref[pl.ds(h, 1), :] - normalized * mean) * inverse).astype(BF16)
+        ga_ref[:, c] = grad
+        behind.state[c, :] = (scaling * dot(q_ref[:, c], grad, 0, 0)).astype(BF16)
+
     def normalize(h):
         c = cols(h)
-        weight = gain_ref[pl.ds(h, 1), :]
-        upstream = cot_ref[:, c].astype(F32)
         normalized = att_ref[:, c] * inverse
-        out_ref[:, c] = (weight * normalized).astype(BF16)
-        gain_part[h] = jnp.sum(upstream * normalized, axis=0, keepdims=True)
-        grad = ((upstream * weight - normalized * mean) * inverse).astype(BF16)
-        ga_ref[:, c] = grad
-        behind.state[c, :] = (scaling * dot(q_ref[:, c], grad, 0, 0)).astype(BF16)
-
-    chunk_loop(0, normalize)
-    behind.send_far(0)
-    chunk_loop(1, normalize)
-    behind.send_far(1)
-    behind.send_near(0)
-    behind.send_near(1)
+        out_ref[:, c] = (gain_ref[pl.ds(h, 1), :] * normalized).astype(BF16)
+
+    def gain_of(h):
+        c = cols(h)
+        gain_part[h] = jnp.sum(cot_ref[:, c].astype(F32) * (att_ref[:, c] * inverse), axis=0, keepdims=True)
+
+    x, z = seq // RING, lax.rem(seq, RING)
 
     def gain_copy(src, dst, index, axis, peer):
         return pltpu.make_async_remote_copy(
@@ -495,10 +504,36 @@
     def part(j):
         return pl.ds(j * grows, grows)
 
-    @pl.loop(1, n_dp)
-    def _(k):
-        peer = lax.rem(dp + k, n_dp)
-        gain_copy(gain_part.at[part(peer)], gain_r1.at[part(dp)], 0, "dp", peer).start()
+    def added(parts, count):
+        total = parts[part(0)]
+        for j in range(1, count):
+            total = total + parts[part(j)]
+        return total
+
+    def gain_round(src_of, dst, index, axis, me, count, peer_of):
+        @pl.loop(1, count)
+        def _(k):
+            at = lax.rem(me + k, count)
+            gain_copy(src_of(at), dst.at[part(me)], index, axis, peer_of(at)).start()
+
+        rest = pl.ds(0, (count - 1) * grows)
+        return gain_copy(dst.at[rest], dst.at[rest], index, axis, peer_of(lax.rem(me + 1, count)))
+
+    def on_x(at):
+        return at * RING + z
+
+    chunk_loop(0, pull)
+    behind.send_far(0)
+    chunk_loop(1, pull)
+    behind.send_far(1)
+    chunk_loop(0, gain_of)
+    chunk_loop(1, gain_of)
+    behind.send_near(0)
+    behind.send_near(1)
+    first = gain_round(lambda at: gain_part.at[part(at)], gain_r1, 0, "seq", x, n_x, on_x)
+    gain_r1[part(x)] = gain_part[part(x)]
+    chunk_loop(0, normalize)
+    chunk_loop(1, normalize)
 
     store_out = pltpu.make_async_copy(out_ref, out_hbm.at[0], store_sem.at[0])
     store_out.start()
@@ -515,48 +550,34 @@
     chunk_loop(0, grads)
     behind.relay(0)
     behind.relay(1)
+
+    first.wait_recv()
+    total = added(gain_r1, n_x)
+    gain_s2[...] = total
+    gain_r2[part(z)] = total
+    second = gain_round(lambda at: gain_s2, gain_r2, 1, "seq", z, RING, lambda at: x * RING + at)
+
     chunk_loop(1, grads)
     store_gq = pltpu.make_async_copy(gq_ref, gq_hbm.at[0], store_sem.at[1])
     store_gq.start()
 
-    gain_r1[part(dp)] = gain_part[part(dp)]
-    others = pl.ds(0, (n_dp - 1) * grows)
-    first = gain_copy(gain_part.at[others], gain_r1.at[others], 0, "dp", lax.rem(dp + 1, n_dp))
-    first.wait_recv()
-    summed = jnp.zeros((grows, 1, HEAD), F32)
-    for j in range(n_dp):
-        summed = summed + gain_r1[pl.ds(j * grows, grows)]
-    gain_s2[...] = summed
-
-    @pl.loop(1, n_seq)
-    def _(k):
-        peer = lax.rem(seq + k, n_seq)
-        gain_copy(gain_s2, gain_r2.at[pl.ds(seq * grows, grows)], 1, "seq", peer).start()
-
     behind.own(0)
+
+    second.wait_recv()
+    total = added(gain_r2, RING)
+    gain_s3[...] = total
+    gain_r3[part(dp)] = total
+    third = gain_round(lambda at: gain_s3, gain_r3, 2, "dp", dp, n_dp, lambda at: at)
+
     behind.own(1)
     behind.give_near(0)
     behind.give_near(1)
-
     behind.pass_on(0)
     behind.pass_on(1)
 
-    gain_r2[pl.ds(seq * grows, grows)] = summed
-    some = pl.ds(0, (n_seq - 1) * grows)
-    second = gain_copy(gain_r2.at[some], gain_r2.at[some], 1, "seq", lax.rem(seq + 1, n_seq))
-    second.wait_recv()
-
-    def add(j, total):
-        return total + gain_r2[pl.ds(j * grows, grows)]
-
-    total = lax.fori_loop(0, n_seq, add, jnp.zeros((grows, 1, HEAD), F32)) / n_dp
-    gain_r3[part(dp)] = total
-
-    @pl.loop(1, n_dp)
-    def _(k):
-        peer = lax.rem(dp + k, n_dp)
-        gain_copy(gain_r3.at[part(dp)], gain_r3.at[part(dp)], 2, "dp", peer).start()
-
+    third.wait_recv()
+    gain_r4[part(x)] = added(gain_r3, n_dp) / n_dp
+    fourth = gain_round(lambda at: gain_r4.at[part(x)], gain_r4, 3, "seq", x, n_x, on_x)
 
     def finish(h):
         c = cols(h)
@@ -564,18 +585,19 @@
         gk_ref[:, c] = (gk_part[:, c] + dot(v_ref[:, c], suffix, 1, 1)).astype(BF16)
         gv_ref[:, c] = (gv_part[:, c] + dot(k_ref[:, c], suffix, 1, 0)).astype(BF16)
 
+    def put(h):
+        c = cols(h)
+        pltpu.make_async_copy(gk_ref.at[:, c], gk_hbm.at[0, :, c], store_sem.at[2]).start()
+        pltpu.make_async_copy(gv_ref.at[:, c], gv_hbm.at[0, :, c], store_sem.at[3]).start()
+
     for chunk in range(CHUNKS):
         behind.arrive(chunk)
         chunk_loop(chunk, finish)
-    store_gk = pltpu.make_async_copy(gk_ref, gk_hbm.at[0], store_sem.at[2])
-    store_gv = pltpu.make_async_copy(gv_ref, gv_hbm.at[0], store_sem.at[3])
-    store_gk.start()
-    store_gv.start()
-
-    third = gain_copy(gain_r3.at[others], gain_r3.at[others], 2, "dp", lax.rem(dp + 1, n_dp))
-    third.wait_recv()
+        chunk_loop(chunk, put)
+
+    fourth.wait_recv()
     for h in range(HEADS):
-        gain_out[h : h + 1, :] = gain_r3[h]
+        gain_out[h : h + 1, :] = gain_r4[h]
     store_gain = pltpu.make_async_copy(gain_out, gg_hbm, store_sem.at[4])
     store_gain.start()
 
@@ -585,6 +607,9 @@
     first.wait_send()
     second.wait_send()
     third.wait_send()
+    fourth.wait_send()
+    store_gk = pltpu.make_async_copy(gk_ref, gk_hbm.at[0], store_sem.at[2])
+    store_gv = pltpu.make_async_copy(gv_ref, gv_hbm.at[0], store_sem.at[3])
     for store in (store_out, store_gq, store_gk, store_gv, store_gain):
         store.wait()
 
@@ -608,7 +633,7 @@
 
     def per_device(queries, keys, values, gain, cotangent):
         _, tokens, features = queries.shape
-        grows = HEADS // n_dp
+        grows = HEADS * RING // n_seq
         exact = pltpu.VMEM((tokens, features), F32)
         half = pltpu.VMEM((tokens, features), BF16)
         big = jax.ShapeDtypeStruct(queries.shape, BF16)
@@ -639,15 +664,17 @@
                 pltpu.VMEM((HEADS, 1, HEAD), F32),
                 pltpu.VMEM((HEADS, 1, HEAD), F32),
                 pltpu.VMEM((grows, 1, HEAD), F32),
-                pltpu.VMEM((n_seq * grows, 1, HEAD), F32),
+                pltpu.VMEM((RING * grows, 1, HEAD), F32),
+                pltpu.VMEM((grows, 1, HEAD), F32),
+                pltpu.VMEM((n_dp * grows, 1, HEAD), F32),
                 pltpu.VMEM((HEADS, 1, HEAD), F32),
                 pltpu.VMEM((HEADS, HEAD), F32),
-                pltpu.SemaphoreType.DMA((5,)),
+                pltpu.SemaphoreType.DMA((7,)),
                 pltpu.SemaphoreType.DMA((5,)),
                 pltpu.SemaphoreType.DMA((2, CHUNKS, KINDS)),
                 pltpu.SemaphoreType.DMA((2, CHUNKS, KINDS)),
-                pltpu.SemaphoreType.DMA((3,)),
-                pltpu.SemaphoreType.DMA((3,)),
+                pltpu.SemaphoreType.DMA((4,)),
+                pltpu.SemaphoreType.DMA((4,)),
             ],
             compiler_params=pltpu.CompilerParams(
                 collective_id=0, has_side_effects=True, vmem_limit_bytes=32 * 2**20

time: 66.4 us -> 64.5 us (0.971)
  the two profiles are of different devices: /device:TPU:1 before, /device:TPU:8 now
where the time goes in v4:
time: 64.5 us; the launch traced here: 64.3 us
  Pallas kernels  63.7 us (99%)
    pallas_call x1, Pallas kernels, per_device(): pl.pallas_call(functools.partial(kernel, n_seq, n_dp), out_shape=(big, bi...  62.3 us
    pallas_call x1, Pallas kernels, per_device(): pl.pallas_call(hand_out, out_shape=(big, big, big, big, small), in_specs=...  1.36 us

profile of v4, /device:TPU:8, one launch (start us, length us, event | category | flops | bytes accessed | tf_op | source)
XLA Modules:
  0.0 64.3 jit_solution(1548145555351554173)
XLA Ops:
  0.6 62.3 %shard_map.92 = (bf16[1,128,2048]{2,1,0:T(8,128)(2,1)S(1)}, bf16[1,128,2048]{2,1,0:T(8,128)(2,1)S(1)}, bf16[1,128,2048]{2,1,0:T(8,128)(2,1)S(1)}, bf16[1,128,2048]{2,1,0:T(8,128)(2,1)S(1)}, f32[16,128]{1,0:T(8,128)S(1)}) custom-call(bf16[1,128,2048]{2,1,0:T(8,128)(2,1)} %q_hbm.1, bf16[1,128,2048]{2,1,0:T(8,128)(2,1)} %k_hbm.1, bf16[1,128,2048]{2,1,0:T(8,128)(2,1)} %v_hbm.1, ...), custom_call_target="tpu_custom_call" | custom-call | tf_op jit(solution)/shard_map/pallas_call | solution.py:641
  63.0 1.4 %shard_map.93 = (bf16[1,128,2048]{2,1,0:T(8,128)(2,1)}, bf16[1,128,2048]{2,1,0:T(8,128)(2,1)}, bf16[1,128,2048]{2,1,0:T(8,128)(2,1)}, bf16[1,128,2048]{2,1,0:T(8,128)(2,1)}, f32[16,128]{1,0:T(8,128)}) custom-call(bf16[1,128,2048]{2,1,0:T(8,128)(2,1)S(1)} %get-tuple-element.15.refs_0_, bf16[1,128,2048]{2,1,0:T(8,128)(2,1)S(1)} %get-tuple-element.16.refs_1_, ...), custom_call_target="tpu_custom_call" | custom-call | tf_op jit(solution)/shard_map/pallas_call | solution.py:684

commit v5 on v4

--- a/solution.py
+++ b/solution.py
@@ -445,8 +445,8 @@
     ahead.relay(1)
     chunk_loop(1, local_of)
     ahead.own(0)
+    ahead.give_near(0)
     ahead.own(1)
-    ahead.give_near(0)
     ahead.give_near(1)
     ahead.pass_on(0)
     ahead.pass_on(1)
@@ -562,6 +562,7 @@
     store_gq.start()
 
     behind.own(0)
+    behind.give_near(0)
 
     second.wait_recv()
     total = added(gain_r2, RING)
@@ -570,7 +571,6 @@
     third = gain_round(lambda at: gain_s3, gain_r3, 2, "dp", dp, n_dp, lambda at: at)
 
     behind.own(1)
-    behind.give_near(0)
     behind.give_near(1)
     behind.pass_on(0)
     behind.pass_on(1)

time: 64.5 us -> 65.1 us (level)
  the two profiles are of different devices: /device:TPU:8 before, /device:TPU:2 now
where the time goes in v5:
time: 65.1 us; the launch traced here: 64.9 us
  Pallas kernels  64.3 us (99%)
    pallas_call x1, Pallas kernels, per_device(): pl.pallas_call(functools.partial(kernel, n_seq, n_dp), out_shape=(big, bi...  62.9 us
    pallas_call x1, Pallas kernels, per_device(): pl.pallas_call(hand_out, out_shape=(big, big, big, big, small), in_specs=...  1.36 us

profile of v5, /device:TPU:2, one launch (start us, length us, event | category | flops | bytes accessed | tf_op | source)
XLA Modules:
  0.0 64.9 jit_solution(13108748461725536220)
XLA Ops:
  0.6 62.9 %shard_map.92 = (bf16[1,128,2048]{2,1,0:T(8,128)(2,1)S(1)}, bf16[1,128,2048]{2,1,0:T(8,128)(2,1)S(1)}, bf16[1,128,2048]{2,1,0:T(8,128)(2,1)S(1)}, bf16[1,128,2048]{2,1,0:T(8,128)(2,1)S(1)}, f32[16,128]{1,0:T(8,128)S(1)}) custom-call(bf16[1,128,2048]{2,1,0:T(8,128)(2,1)} %q_hbm.1, bf16[1,128,2048]{2,1,0:T(8,128)(2,1)} %k_hbm.1, bf16[1,128,2048]{2,1,0:T(8,128)(2,1)} %v_hbm.1, ...), custom_call_target="tpu_custom_call" | custom-call | tf_op jit(solution)/shard_map/pallas_call | solution.py:641
  63.6 1.4 %shard_map.93 = (bf16[1,128,2048]{2,1,0:T(8,128)(2,1)}, bf16[1,128,2048]{2,1,0:T(8,128)(2,1)}, bf16[1,128,2048]{2,1,0:T(8,128)(2,1)}, bf16[1,128,2048]{2,1,0:T(8,128)(2,1)}, f32[16,128]{1,0:T(8,128)}) custom-call(bf16[1,128,2048]{2,1,0:T(8,128)(2,1)S(1)} %get-tuple-element.15.refs_0_, bf16[1,128,2048]{2,1,0:T(8,128)(2,1)S(1)} %get-tuple-element.16.refs_1_, ...), custom_call_target="tpu_custom_call" | custom-call | tf_op jit(solution)/shard_map/pallas_call | solution.py:684
